TPU v7x, 128 devices: a whole 4x4x4 slice. The times are simulated.
128 devices in a mesh: grp: 4 (over y), row: 32 (over z, x, core).
Axes of the slice: x: 4, y: 4, z: 4, core: 2. Of those that a mesh axis runs over, the one named last changes fastest.
Arguments:
- feats: bfloat16 [65536, 512], P(('grp', 'row')), may hold values from -6 to 6
- tile_vals: bfloat16 [12288, 128, 128], P(('grp', 'row')), may hold values from -0.1875 to 0.1875
- tile_rows: int32 [12288], P(('grp', 'row')), may hold values from 0 to 15, as said below
- tile_slots: int32 [12288], P(('grp', 'row')), may hold values from 0 to 31, as said below
- tile_count: int32 [128], P(('grp', 'row')), may hold values from 32 to 96, as said below
- send_list: int32 [128, 32, 1], P(('grp', 'row')), may hold values from 0 to 3
- w_in: bfloat16 [2, 512, 1024], replicated, may hold values from -0.25 to 0.25
- w_out: bfloat16 [2, 1024, 512], replicated, may hold values from -0.1875 to 0.1875
- cotangent: bfloat16 [65536, 512], P(('grp', 'row')), may hold values from -6 to 6
Outputs:
- feat_grad: bfloat16 [65536, 512], P(('grp', 'row'))
- w_in_grad: float32 [2, 512, 1024], P(None, ('grp', 'row'))
- w_out_grad: float32 [2, 1024, 512], P(None, ('grp', 'row'))
Inputs may be any that keep to these rules, and one draw needn't show every extreme that they name: send_list[d, r, c] is the own block (0 to 3) that device d sends as its c-th to the device at row index r of its grp. p = tile_rows[d * 96 + t] names block p % 4 of the device at grp index p // 4 and d's row index; each of the 16 values stands among the first 16 tiles of every device. `tile_slots`: slot s is the block that the device at row index s of the same grp sends to this device; each of the 32 slots stands among the first 32 tiles of every device. Only the first tile_count[d] tiles of device d are used; at least one device uses all 96.
All inputs are finite; a program needn't handle non-finite values.
Results may differ from a plain program's by a relative error of at most 0.017.
Values may be sent and summed in bfloat16 or wider, within the bound.
No kernel may reach another device: no remote copies, remote signals or barrier semaphores. Data moves between devices by JAX's collectives and lax.ppermute only.
A program may use at most 128 MiB of HBM per device.

v0:
```python
import jax
import jax.numpy as jnp
from jax import lax
from jax.sharding import Mesh
from jax.sharding import PartitionSpec as P

ROW = ("row_0", "row_1", "row_2")
GRP_ROW = ("grp", "row_0", "row_1", "row_2")


eps = 1e-06
tile_group = 32


def in_blocks(value, dim, length):
    dims = value.shape
    parts = value.reshape(*dims[:dim], length, dims[dim] // length, *dims[dim + 1 :])
    return jnp.moveaxis(parts, dim, 0)


def summed_on_arrival(value, axis, dim):
    parts = in_blocks(value, dim, lax.axis_size(axis))
    arrived = lax.all_to_all(parts, axis, split_axis=0, concat_axis=0, tiled=True)
    return arrived.astype(jnp.float32).sum(axis=0)


def copy_for_each(value, axis):
    length = lax.axis_size(axis)
    return lax.all_to_all(
        jnp.broadcast_to(value[None], (length, *value.shape)), axis, 0, 0, tiled=True
    )


def laid_out(parts, dim):
    dims = list(parts.shape[1:])
    dims[dim] *= parts.shape[0]
    return jnp.moveaxis(parts, 0, dim).reshape(dims)


def collect(value, axis, dim):
    parts = copy_for_each(value, axis)
    return laid_out(parts, dim)


def summed_on_arrival_2(value, axis, dim):
    parts = in_blocks(value, dim, lax.axis_size(axis))
    arrived = lax.all_to_all(parts, axis, split_axis=0, concat_axis=0, tiled=True)
    return arrived.sum(axis=0)


def sum_in_two_steps(value, axes, dim):
    far, near = axes
    parts = in_blocks(value, dim, lax.axis_size(far))
    nearer = summed_on_arrival_2(parts, near, dim + 1)
    arrived = lax.all_to_all(nearer, far, split_axis=0, concat_axis=0, tiled=True)
    return arrived.sum(axis=0)


def forward_tiles(slot_data, tile_vals, tile_rows, tile_slots, count, panel_len):
    tile_len = slot_data.shape[1]
    width = slot_data.shape[2]
    turn_count = (count + tile_group - 1) // tile_group

    def forward_advance(index, totals):
        offset = index * tile_group
        tile_set = lax.dynamic_slice_in_dim(tile_vals, offset, tile_group, 0)
        row_ids = lax.dynamic_slice_in_dim(tile_rows, offset, tile_group, 0)
        slot_ids = lax.dynamic_slice_in_dim(tile_slots, offset, tile_group, 0)
        live_mask = (offset + jnp.arange(tile_group, dtype=jnp.int32) < count).astype(jnp.float32)
        sources = jnp.take(slot_data, slot_ids, axis=0)
        products = jnp.einsum("tij,tjd->tid", tile_set, sources, preferred_element_type=jnp.float32)
        return totals.at[row_ids].add(products * live_mask[:, None, None])

    empty = jnp.zeros((panel_len, tile_len, width), jnp.float32)
    return lax.fori_loop(0, turn_count, forward_advance, empty)


def backward_tiles(panel_grad, tile_vals, tile_rows, tile_slots, count, slot_count):
    tile_len = panel_grad.shape[1]
    width = panel_grad.shape[2]
    turn_count = (count + tile_group - 1) // tile_group

    def backward_advance(index, totals):
        offset = index * tile_group
        tile_set = lax.dynamic_slice_in_dim(tile_vals, offset, tile_group, 0)
        row_ids = lax.dynamic_slice_in_dim(tile_rows, offset, tile_group, 0)
        slot_ids = lax.dynamic_slice_in_dim(tile_slots, offset, tile_group, 0)
        live_mask = (offset + jnp.arange(tile_group, dtype=jnp.int32) < count).astype(jnp.float32)
        sources = jnp.take(panel_grad, row_ids, axis=0)
        products = jnp.einsum("tji,tjd->tid", tile_set, sources, preferred_element_type=jnp.float32)
        return totals.at[slot_ids].add(products * live_mask[:, None, None])

    empty = jnp.zeros((slot_count, tile_len, width), jnp.float32)
    return lax.fori_loop(0, turn_count, backward_advance, empty)


def body(feats, tile_vals, tile_rows, tile_slots, tile_count, send_list, w_in, w_out, cotangent):
    row_count = lax.axis_size(ROW)
    grp_count = lax.axis_size("grp")
    node_count = feats.shape[0]
    width = feats.shape[1]
    tile_len = tile_vals.shape[1]
    per_dev = node_count // tile_len
    slot_cap = send_list.shape[2]
    slot_count = row_count * slot_cap
    panel_len = grp_count * per_dev
    layer_count = w_in.shape[0]
    count = tile_count[0]
    outgoing = send_list[0].reshape(slot_count)
    send_hot = (outgoing[:, None] == jnp.arange(per_dev, dtype=jnp.int32)[None, :]).astype(
        jnp.bfloat16
    )
    factor = float(node_count * lax.axis_size(GRP_ROW)) ** (-0.5)
    contract_rows = (((0,), (0,)), ((), ()))
    contract_cols = (((1,), (1,)), ((), ()))
    hidden = feats
    saved = []
    for layer in range(layer_count):
        own_blocks = hidden.reshape(per_dev, tile_len, width)
        outgoing_blocks = jnp.take(own_blocks, outgoing, axis=0).reshape(
            row_count, slot_cap, tile_len, width
        )
        slot_data = lax.all_to_all(
            outgoing_blocks, ROW, split_axis=0, concat_axis=0, tiled=True
        ).reshape(slot_count, tile_len, width)
        partial_value = forward_tiles(slot_data, tile_vals, tile_rows, tile_slots, count, panel_len)
        message = summed_on_arrival(
            partial_value.reshape(panel_len * tile_len, width).astype(jnp.bfloat16), "grp", 0
        )
        summed = message + hidden.astype(jnp.float32)
        norm_scale = lax.rsqrt(jnp.mean(summed * summed, axis=-1, keepdims=True) + eps)
        normed = summed * norm_scale
        normed_b = normed.astype(jnp.bfloat16)
        pre_act = jnp.dot(normed_b, w_in[layer], preferred_element_type=jnp.float32)
        activated = jax.nn.silu(pre_act).astype(jnp.bfloat16)
        update = jnp.dot(activated, w_out[layer], preferred_element_type=jnp.float32)
        saved.append((norm_scale, normed, normed_b, pre_act, activated))
        hidden = (hidden.astype(jnp.float32) + update).astype(jnp.bfloat16)
    grad_now = cotangent
    in_local = [None] * layer_count
    out_local = [None] * layer_count
    for layer in reversed(range(layer_count)):
        norm_scale, normed, normed_b, pre_act, activated = saved[layer]
        out_term = lax.dot_general(
            activated, grad_now, contract_rows, preferred_element_type=jnp.float32
        )
        d_act = lax.dot_general(
            grad_now, w_out[layer], contract_cols, preferred_element_type=jnp.float32
        )
        sigma = jax.nn.sigmoid(pre_act)
        d_pre = (d_act * sigma * (1.0 + pre_act * (1.0 - sigma))).astype(jnp.bfloat16)
        in_term = lax.dot_general(
            normed_b, d_pre, contract_rows, preferred_element_type=jnp.float32
        )
        in_local[layer] = in_term
        out_local[layer] = out_term
        d_unit = lax.dot_general(
            d_pre, w_in[layer], contract_cols, preferred_element_type=jnp.float32
        )
        d_summed = norm_scale * (
            d_unit - normed * jnp.mean(d_unit * normed, axis=-1, keepdims=True)
        )
        d_summed_b = d_summed.astype(jnp.bfloat16)
        panel_grad = collect(d_summed_b, "grp", 0).reshape(panel_len, tile_len, width)
        per_slot = backward_tiles(panel_grad, tile_vals, tile_rows, tile_slots, count, slot_count)
        per_slot = per_slot.astype(jnp.bfloat16).reshape(row_count, slot_cap, tile_len, width)
        returned = lax.all_to_all(per_slot, ROW, split_axis=0, concat_axis=0, tiled=True).reshape(
            slot_count, tile_len, width
        )
        returned_sum = jnp.einsum(
            "sb,sid->bid", send_hot, returned, preferred_element_type=jnp.float32
        )
        grad_now = (
            grad_now.astype(jnp.float32) + d_summed + returned_sum.reshape(node_count, width)
        ).astype(jnp.bfloat16)
    in_sums, out_sums = (
        sum_in_two_steps(jnp.stack(in_local), (("grp", "row_0", "row_1"), "row_2"), 1),
        sum_in_two_steps(jnp.stack(out_local), (("grp", "row_0", "row_1"), "row_2"), 1),
    )
    w_in_grad = in_sums * factor
    w_out_grad = out_sums * factor
    return (grad_now, w_in_grad, w_out_grad)


def solution(mesh):
    torus = Mesh(
        mesh.devices.reshape(mesh.shape["grp"], 4, 4, 2), ("grp", "row_0", "row_1", "row_2")
    )
    in_specs = (
        P(GRP_ROW, None),
        P(GRP_ROW, None, None),
        P(GRP_ROW),
        P(GRP_ROW),
        P(GRP_ROW),
        P(GRP_ROW, None, None),
        P(),
        P(),
        P(GRP_ROW, None),
    )
    out_specs = (P(GRP_ROW, None), P(None, GRP_ROW, None), P(None, GRP_ROW, None))
    return jax.shard_map(body, mesh=torus, in_specs=in_specs, out_specs=out_specs, check_vma=False)
```

profile of v0, /device:TPU:32, one launch (start us, length us, event | category | flops | bytes accessed | tf_op | source)
XLA Modules:
  0.0 838.9 jit_solution(13179465545937784848)
XLA Ops:
  2.0 3.8 gather_fusion.4
  5.8 4.6 select_bitcast_fusion.1
  10.3 8.1 all-to-all-start
  19.2 50.4 %all-to-all-done = bf16[32,1,128,512]{3,2,1,0:T(8,128)(2,1)} async-done(((bf16[32,1,128,512]{3,2,1,0:T(8,128)(2,1)}), bf16[32,1,128,512]{3,2,1,0:T(8,128)(2,1)}, u32[]{:S(2)}, u32[]{:S(2)}) %all-to-all-start) | async-done | bytes 4194336 | tf_op jit(solution)/shard_map/all_to_all | solution.py:123
  72.0 31.3 %while.40 = (s32[]{:T(128)}, f32[16,128,512]{2,1,0:T(8,128)}, s32[]{:T(128)}, s32[96]{0:T(128)S(1)}, bf16[96,128,128]{2,1,0:T(8,128)(2,1)}, /*index=5*/s32[96]{0...) while((s32[]{:T(128)}, f32[16,128,512]{2,1,0:T(8,128)}, ...), condition=%wide.region_2.5_spmd, body=%wide.region_0.4_spmd.sunk | while | flops 543163776 | bytes 47191416 | solution.py:75
  72.8 4.9 gather_fusion
  77.7 7.1 broadcast_multiply_fusion.12
  84.9 18.5 %scatter_fusion = f32[16,128,512]{2,1,0:T(8,128)} fusion(f32[16,128,512]{2,1,0:T(8,128)} %get-tuple-element.563, s32[32]{0:T(128)S(1)} %compare_select_fusion.17, f32[32,128,512]{2,1,0:T(8,128)} %broadcast_multiply_fusion.12), kind=kCustom, calls=%fused_computation.6.clone.1 | custom fusion | flops 2097152 | bytes 25165952 | tf_op jit(solution)/shard_map/while/body/scatter-add | solution.py:72
  105.9 52.0 %all_to_all.60 = bf16[4,512,512]{2,1,0:T(8,128)(2,1)S(1)} all-to-all(bf16[4,512,512]{2,1,0:T(8,128)(2,1)S(1)} %bitcast.100), channel_id=1, replica_groups=mesh['grp'=4,'row_0'=4,'row_1'=4,'row_2'=2] {'grp'}, dimensions={0} | all-to-all | bytes 4194304 | tf_op jit(solution)/shard_map/all_to_all | solution.py:23
  164.8 4.6 select_bitcast_fusion
  169.4 35.2 %all-to-all-start.2 = ((bf16[32,1,128,512]{3,2,1,0:T(8,128)(2,1)}), bf16[32,1,128,512]{3,2,1,0:T(8,128)(2,1)}, u32[]{:S(2)}, u32[]{:S(2)}) async-start(bf16[32,1,128,512]{3,2,1,0:T(8,128)(2,1)} %select_bitcast_fusion), calls=%async_computation.2 | async-start | bytes 8388608 | tf_op jit(solution)/shard_map/all_to_all | solution.py:123
  204.6 51.1 %all-to-all-done.2 = bf16[32,1,128,512]{3,2,1,0:T(8,128)(2,1)} async-done(((bf16[32,1,128,512]{3,2,1,0:T(8,128)(2,1)}), bf16[32,1,128,512]{3,2,1,0:T(8,128)(2,1)}, u32[]{:S(2)}, u32[]{:S(2)}) %all-to-all-start.2) | async-done | bytes 4194336 | tf_op jit(solution)/shard_map/all_to_all | solution.py:123
  258.1 31.3 %while.41 = (s32[]{:T(128)}, f32[16,128,512]{2,1,0:T(8,128)}, s32[]{:T(128)}, s32[96]{0:T(128)S(1)}, bf16[96,128,128]{2,1,0:T(8,128)(2,1)}, /*index=5*/s32[96]{0...) while((s32[]{:T(128)}, f32[16,128,512]{2,1,0:T(8,128)}, ...), condition=%wide.region_7.10_spmd, body=%wide.region_5.9_spmd.sunk | while | flops 543163776 | bytes 47191416 | solution.py:75
  258.9 4.9 gather_fusion.1
  263.8 7.1 broadcast_multiply_fusion.13
  271.0 18.5 %scatter_fusion.1 = f32[16,128,512]{2,1,0:T(8,128)} fusion(f32[16,128,512]{2,1,0:T(8,128)} %get-tuple-element.599, s32[32]{0:T(128)S(1)} %compare_select_fusion.18, f32[32,128,512]{2,1,0:T(8,128)} %broadcast_multiply_fusion.13), kind=kCustom, calls=%fused_computation.8.clone.1 | custom fusion | flops 2097152 | bytes 25165952 | tf_op jit(solution)/shard_map/while/body/scatter-add | solution.py:72
  292.0 50.2 %all_to_all.61 = bf16[4,512,512]{2,1,0:T(8,128)(2,1)S(1)} all-to-all(bf16[4,512,512]{2,1,0:T(8,128)(2,1)S(1)} %bitcast.101), channel_id=1, replica_groups=mesh['grp'=4,'row_0'=4,'row_1'=4,'row_2'=2] {'grp'}, dimensions={0} | all-to-all | bytes 4194304 | tf_op jit(solution)/shard_map/all_to_all | solution.py:23
  349.6 3.6 all-to-all-start.4
  353.2 4.6 copy.54
  357.8 22.1 %all-to-all-done.4 = bf16[4,512,512]{2,1,0:T(8,128)(2,1)S(1)} async-done(((bf16[4,512,512]{2,1,0:T(8,128)(2,1)}), bf16[4,512,512]{2,1,0:T(8,128)(2,1)S(1)}, u32[]{:S(2)}, u32[]{:S(2)}) %all-to-all-start.4) | async-done | bytes 2097184 | tf_op jit(solution)/shard_map/all_to_all | solution.py:29
  379.9 4.3 broadcast.121.clone
  384.2 29.5 %while.42 = (s32[]{:T(128)}, f32[32,128,512]{2,1,0:T(8,128)}, s32[]{:T(128)}, s32[96]{0:T(128)S(1)}, bf16[96,128,128]{1,2,0:T(8,128)(2,1)}, /*index=5*/s32[96]{0...) while((s32[]{:T(128)}, f32[32,128,512]{2,1,0:T(8,128)}, ...), condition=%wide.region_13.17_spmd, body=%wide.region_11.16_spmd.sunk | while | flops 543163776 | bytes 47191416 | solution.py:94
  387.7 7.1 broadcast_multiply_fusion.14
  394.9 18.8 %scatter_fusion.2 = f32[32,128,512]{2,1,0:T(8,128)} fusion(f32[32,128,512]{2,1,0:T(8,128)} %get-tuple-element.635, s32[32]{0:T(128)S(1)} %compare_select_fusion.19, f32[32,128,512]{2,1,0:T(8,128)} %broadcast_multiply_fusion.14), kind=kCustom, calls=%fused_computation.7.clone.1 | custom fusion | flops 2097152 | bytes 25165952 | tf_op jit(solution)/shard_map/while/body/scatter-add | solution.py:91
  413.7 5.9 convert_bitcast_fusion.1
  419.7 91.0 %all-to-all-start.5 = ((bf16[32,1,128,512]{3,2,1,0:T(8,128)(2,1)}), bf16[32,1,128,512]{3,2,1,0:T(8,128)(2,1)}, u32[]{:S(2)}, u32[]{:S(2)}) async-start(bf16[32,1,128,512]{3,2,1,0:T(8,128)(2,1)} %convert_bitcast_fusion.1), calls=%async_computation.5 | async-start | bytes 8388608 | tf_op jit(solution)/shard_map/all_to_all | solution.py:167
  516.2 45.3 %all-to-all-done.5 = bf16[32,1,128,512]{3,2,1,0:T(8,128)(2,1)} async-done(((bf16[32,1,128,512]{3,2,1,0:T(8,128)(2,1)}), bf16[32,1,128,512]{3,2,1,0:T(8,128)(2,1)}, u32[]{:S(2)}, u32[]{:S(2)}) %all-to-all-start.5) | async-done | bytes 4194336 | tf_op jit(solution)/shard_map/all_to_all | solution.py:167
  561.4 4.6 fusion.38
  576.8 6.0 all-to-all-start.10
  586.1 4.7 copy.64
  591.1 11.9 %all_to_all.62 = f32[2,64,2,4,1024]{4,3,1,2,0:T(4,128)} all-to-all(f32[2,64,2,4,1024]{4,3,1,2,0:T(4,128)} %copy.64), channel_id=1, replica_groups=mesh['grp'=4,'row_0'=4,'row_1'=4,'row_2'=2] {'row_2'}, dimensions={0} | all-to-all | bytes 8388608 | tf_op jit(solution)/shard_map/all_to_all | solution.py:47
  604.5 3.6 all-to-all-start.6
  608.1 4.3 reduce_sum.98
  612.4 3.1 copy.71
  615.5 19.5 %all-to-all-done.6 = bf16[4,512,512]{2,1,0:T(8,128)(2,1)S(1)} async-done(((bf16[4,512,512]{2,1,0:T(8,128)(2,1)}), bf16[4,512,512]{2,1,0:T(8,128)(2,1)S(1)}, u32[]{:S(2)}, u32[]{:S(2)}) %all-to-all-start.6) | async-done | bytes 2097184 | tf_op jit(solution)/shard_map/all_to_all | solution.py:29
  635.0 8.2 all-to-all-start.11
  643.2 5.6 reduce_sum.96
  648.8 3.3 copy.66
  652.1 20.4 %all-to-all-done.11 = f32[64,2,8,512]{3,2,1,0:T(8,128)} async-done(((f32[64,2,8,512]{3,2,1,0:T(8,128)}), f32[64,2,8,512]{3,2,1,0:T(8,128)}, u32[]{:S(2)}, u32[]{:S(2)}) %all-to-all-start.11) | async-done | bytes 2097184 | tf_op jit(solution)/shard_map/all_to_all | solution.py:55
  672.4 6.4 all-to-all-start.9
  678.8 4.3 broadcast.121
  683.1 29.6 %while.43 = (s32[]{:T(128)}, f32[32,128,512]{2,1,0:T(8,128)}, s32[]{:T(128)}, s32[96]{0:T(128)S(1)}, bf16[96,128,128]{1,2,0:T(8,128)(2,1)}, /*index=5*/s32[96]{0...) while((s32[]{:T(128)}, f32[32,128,512]{2,1,0:T(8,128)}, ...), condition=%wide.region_17.21_spmd, body=%wide.region_15.20_spmd.sunk | while | flops 543163776 | bytes 47191416 | solution.py:94
  686.7 7.1 broadcast_multiply_fusion.15
  693.9 18.8 %scatter_fusion.3 = f32[32,128,512]{2,1,0:T(8,128)} fusion(f32[32,128,512]{2,1,0:T(8,128)} %get-tuple-element.671, s32[32]{0:T(128)S(1)} %compare_select_fusion.20, f32[32,128,512]{2,1,0:T(8,128)} %broadcast_multiply_fusion.15), kind=kCustom, calls=%fused_computation.9.clone.1 | custom fusion | flops 2097152 | bytes 25165952 | tf_op jit(solution)/shard_map/while/body/scatter-add | solution.py:91
  712.7 5.9 convert_bitcast_fusion
  718.7 62.8 %all-to-all-start.7 = ((bf16[32,1,128,512]{3,2,1,0:T(8,128)(2,1)}), bf16[32,1,128,512]{3,2,1,0:T(8,128)(2,1)}, u32[]{:S(2)}, u32[]{:S(2)}) async-start(bf16[32,1,128,512]{3,2,1,0:T(8,128)(2,1)} %convert_bitcast_fusion), calls=%async_computation.7 | async-start | bytes 8388608 | tf_op jit(solution)/shard_map/all_to_all | solution.py:167
  786.5 46.1 %all-to-all-done.7 = bf16[32,1,128,512]{3,2,1,0:T(8,128)(2,1)} async-done(((bf16[32,1,128,512]{3,2,1,0:T(8,128)(2,1)}), bf16[32,1,128,512]{3,2,1,0:T(8,128)(2,1)}, u32[]{:S(2)}, u32[]{:S(2)}) %all-to-all-start.7) | async-done | bytes 4194336 | tf_op jit(solution)/shard_map/all_to_all | solution.py:167
  832.6 4.6 fusion.36
  (134 shorter events, 62.0 us)
Async XLA Ops:
  10.3 59.2 %all-to-all-start = ((bf16[32,1,128,512]{3,2,1,0:T(8,128)(2,1)}), bf16[32,1,128,512]{3,2,1,0:T(8,128)(2,1)}, u32[]{:S(2)}, u32[]{:S(2)}) async-start(bf16[32,1,128,512]{3,2,1,0:T(8,128)(2,1)} %select_bitcast_fusion.1), calls=%async_computation | async-start | bytes 8388608 | tf_op jit(solution)/shard_map/all_to_all | solution.py:123
  18.5 53.6 %copy-start.28 = (s32[96]{0:T(128)S(1)}, s32[96]{0:T(128)}, u32[]{:S(2)}) copy-start(s32[96]{0:T(128)} %param.26) | copy-start | bytes 1156
  18.5 53.6 %copy-start.29 = (s32[96]{0:T(128)S(1)}, s32[96]{0:T(128)}, u32[]{:S(2)}) copy-start(s32[96]{0:T(128)} %param.25) | copy-start | bytes 1156
  105.8 52.3 %copy-start = (bf16[512,512]{1,0:T(8,128)(2,1)S(1)}, bf16[512,512]{1,0:T(8,128)(2,1)}, u32[]{:S(2)}) copy-start(bf16[512,512]{1,0:T(8,128)(2,1)} %param.23) | copy-start | bytes 1572868
  157.8 2.0 copy-start.14
  158.2 3.2 copy-start.2
  158.2 2.5 copy-start.33
  158.4 0.6 copy-start.30
  159.0 0.8 copy-start.8
  160.6 1.4 copy-start.16
  169.4 86.3 %all-to-all-start.2 = ((bf16[32,1,128,512]{3,2,1,0:T(8,128)(2,1)}), bf16[32,1,128,512]{3,2,1,0:T(8,128)(2,1)}, u32[]{:S(2)}, u32[]{:S(2)}) async-start(bf16[32,1,128,512]{3,2,1,0:T(8,128)(2,1)} %select_bitcast_fusion), calls=%async_computation.2 | async-start | bytes 8388608 | tf_op jit(solution)/shard_map/all_to_all | solution.py:123
  342.5 4.4 copy-start.5
  342.5 1.4 copy-start.25
  342.5 2.1 copy-start.34
  344.6 1.3 copy-start.18
  345.9 1.0 copy-start.23
  346.7 1.0 copy-start.12
  349.6 30.4 %all-to-all-start.4 = ((bf16[4,512,512]{2,1,0:T(8,128)(2,1)}), bf16[4,512,512]{2,1,0:T(8,128)(2,1)S(1)}, u32[]{:S(2)}, u32[]{:S(2)}) async-start(bf16[4,512,512]{2,1,0:T(8,128)(2,1)} %broadcast_in_dim.60), calls=%async_computation.4 | async-start | bytes 4194304 | tf_op jit(solution)/shard_map/all_to_all | solution.py:29
  419.6 91.0 %copy-start.24 = (bf16[512,1024]{1,0:T(8,128)(2,1)S(1)}, bf16[512,1024]{1,0:T(8,128)(2,1)}, u32[]{:S(2)}) copy-start(bf16[512,1024]{1,0:T(8,128)(2,1)} %copy-done.23) | copy-start | bytes 3145732
  419.7 141.8 %all-to-all-start.5 = ((bf16[32,1,128,512]{3,2,1,0:T(8,128)(2,1)}), bf16[32,1,128,512]{3,2,1,0:T(8,128)(2,1)}, u32[]{:S(2)}, u32[]{:S(2)}) async-start(bf16[32,1,128,512]{3,2,1,0:T(8,128)(2,1)} %convert_bitcast_fusion.1), calls=%async_computation.5 | async-start | bytes 8388608 | tf_op jit(solution)/shard_map/all_to_all | solution.py:167
  510.6 3.4 copy-start.19
  510.7 3.4 copy-start.26
  514.0 47.4 %copy-start.32 = (s32[1,32,1]{1,2,0:T(1,128)S(1)}, s32[1,32,1]{1,2,0:T(1,128)}, u32[]{:S(2)}) copy-start(s32[1,32,1]{1,2,0:T(1,128)} %param.28) | copy-start | bytes 388
  516.1 50.2 %copy-start.6 = (f32[512,512]{1,0:T(8,128)S(1)}, f32[512,512]{1,0:T(8,128)}, u32[]{:S(2)}) copy-start(f32[512,512]{1,0:T(8,128)} %copy-done.5) | copy-start | bytes 3145732
  516.1 50.2 %copy-start.13 = (f32[512,512]{1,0:T(8,128)S(1)}, f32[512,512]{1,0:T(8,128)}, u32[]{:S(2)}) copy-start(f32[512,512]{1,0:T(8,128)} %copy-done.12) | copy-start | bytes 3145732
  516.2 50.2 %copy-start.27 = (bf16[512,512]{1,0:T(8,128)(2,1)S(1)}, bf16[512,512]{1,0:T(8,128)(2,1)}, u32[]{:S(2)}) copy-start(bf16[512,512]{1,0:T(8,128)(2,1)} %param.31) | copy-start | bytes 1572868
  566.0 1.6 copy-start.17
  567.6 0.8 copy-start.21
  567.6 1.8 copy-start.35
  569.4 1.1 copy-start.9
  569.4 3.2 copy-start.1
  569.4 3.2 copy-start.3
  569.4 3.2 copy-start.15
  569.4 3.2 copy-start.31
  570.5 2.9 copy-start.20
  573.4 17.4 %copy-start.10 = (f32[512,512]{1,0:T(8,128)}, f32[512,512]{1,0:T(8,128)S(1)}, u32[]{:S(2)}) copy-start(f32[512,512]{1,0:T(8,128)S(1)} %get-tuple-element.325) | copy-start | bytes 3145732
  576.8 14.3 %all-to-all-start.10 = ((f32[2,64,2,8,512]{4,3,1,2,0:T(8,128)}), f32[2,64,2,8,512]{4,3,1,2,0:T(8,128)}, u32[]{:S(2)}, u32[]{:S(2)}) async-start(f32[2,64,2,8,512]{4,3,1,2,0:T(8,128)} %copy.69), calls=%async_computation.10 | async-start | bytes 8388608 | tf_op jit(solution)/shard_map/all_to_all | solution.py:47
  582.8 3.0 copy-start.7
  604.5 30.5 %all-to-all-start.6 = ((bf16[4,512,512]{2,1,0:T(8,128)(2,1)}), bf16[4,512,512]{2,1,0:T(8,128)(2,1)S(1)}, u32[]{:S(2)}, u32[]{:S(2)}) async-start(bf16[4,512,512]{2,1,0:T(8,128)(2,1)} %broadcast_in_dim.61), calls=%async_computation.6 | async-start | bytes 4194304 | tf_op jit(solution)/shard_map/all_to_all | solution.py:29
  635.0 37.4 %all-to-all-start.11 = ((f32[64,2,8,512]{3,2,1,0:T(8,128)}), f32[64,2,8,512]{3,2,1,0:T(8,128)}, u32[]{:S(2)}, u32[]{:S(2)}) async-start(f32[64,2,8,512]{3,2,1,0:T(8,128)} %copy.71), calls=%async_computation.11 | async-start | bytes 4194304 | tf_op jit(solution)/shard_map/all_to_all | solution.py:55
  672.4 46.3 %all-to-all-start.9 = ((f32[64,2,4,1024]{3,2,1,0:T(4,128)}), f32[64,2,4,1024]{3,2,1,0:T(4,128)}, u32[]{:S(2)}, u32[]{:S(2)}) async-start(f32[64,2,4,1024]{3,2,1,0:T(4,128)} %copy.66), calls=%async_computation.9 | async-start | bytes 4194304 | tf_op jit(solution)/shard_map/all_to_all | solution.py:55
  718.7 113.9 %all-to-all-start.7 = ((bf16[32,1,128,512]{3,2,1,0:T(8,128)(2,1)}), bf16[32,1,128,512]{3,2,1,0:T(8,128)(2,1)}, u32[]{:S(2)}, u32[]{:S(2)}) async-start(bf16[32,1,128,512]{3,2,1,0:T(8,128)(2,1)} %convert_bitcast_fusion), calls=%async_computation.7 | async-start | bytes 8388608 | tf_op jit(solution)/shard_map/all_to_all | solution.py:167
  785.2 52.3 %copy-start.4 = (f32[512,512]{1,0:T(8,128)S(1)}, f32[512,512]{1,0:T(8,128)}, u32[]{:S(2)}) copy-start(f32[512,512]{1,0:T(8,128)} %copy-done.2) | copy-start | bytes 3145732
  785.2 52.3 %copy-start.11 = (f32[512,512]{1,0:T(8,128)S(1)}, f32[512,512]{1,0:T(8,128)}, u32[]{:S(2)}) copy-start(f32[512,512]{1,0:T(8,128)} %copy-done.10) | copy-start | bytes 3145732
  785.2 52.3 %copy-start.22 = (bf16[512,512]{1,0:T(8,128)(2,1)S(1)}, bf16[512,512]{1,0:T(8,128)(2,1)}, u32[]{:S(2)}) copy-start(bf16[512,512]{1,0:T(8,128)(2,1)} %copy-done.21) | copy-start | bytes 1572868
where the time goes:
time: 854 us; the launch traced here: 839 us
  waiting for transfers between devices  255 us (30%)
  starting transfers between devices  225 us (26%)
  other arithmetic  125 us (15%)
  blocking collectives  114 us (13%)
  local copies, waits for them, and re-layouts  69 us (8%)
  matrix products  49.3 us (6%)
    all_to_all x2, starting transfers between devices, body(): lax.all_to_all(per_slot, ROW, split_axis=0, concat_axis=0, tiled=True)  154 us
    all_to_all x2, blocking collectives, summed_on_arrival(): lax.all_to_all(parts, axis, split_axis=0, concat_axis=0, tiled=True)  102 us
    all_to_all x2, waiting for transfers between devices, body(): lax.all_to_all(outgoing_blocks, ROW, split_axis=0, concat_axis=0, tiled=T...  101 us
    all_to_all x2, waiting for transfers between devices, body(): lax.all_to_all(per_slot, ROW, split_axis=0, concat_axis=0, tiled=True)  91.4 us
    all_to_all x2, starting transfers between devices, body(): lax.all_to_all(outgoing_blocks, ROW, split_axis=0, concat_axis=0, tiled=T...  43.3 us
    all_to_all x2, waiting for transfers between devices, copy_for_each(): lax.all_to_all(jnp.broadcast_to(value[None], (length, *value.shape)), axi...  41.6 us
    scatter-add x2, other arithmetic, backward_advance(): return totals.at[slot_ids].add(products * live_mask[:, None, None])  37.7 us
    scatter-add x2, other arithmetic, forward_advance(): return totals.at[row_ids].add(products * live_mask[:, None, None])  37 us
  transfers between devices with their start and end apart: 9, of which 7 were waited for; matrix products, arithmetic and copies ran while one was open for 9% of the time, Pallas kernels for 0%

commit v1 on v0

v1 whole, which is shorter than its diff:
```python
import functools

import jax
import jax.numpy as jnp
from jax import lax
from jax.experimental import pallas as pl
from jax.experimental.pallas import tpu as pltpu
from jax.sharding import Mesh
from jax.sharding import PartitionSpec as P

ROW = ("row_0", "row_1", "row_2")
GRP_ROW = ("grp", "row_0", "row_1", "row_2")
FAR = ("grp", "row_0", "row_1")
NEAR = "row_2"

eps = 1e-06
UNROLL = 4


def exchange(value, axis):
    return lax.all_to_all(value, axis, split_axis=0, concat_axis=0, tiled=True)


def pair_table(keys, key_count, sources, count):
    tile_cap = keys.shape[0]
    steps = -(-((tile_cap + key_count) // 2) // UNROLL) * UNROLL
    ids = jnp.arange(tile_cap, dtype=jnp.int32)
    key_ids = jnp.arange(key_count, dtype=jnp.int32)
    live = ids < count
    held = (keys[:, None] == key_ids[None, :]) & live[:, None]
    per_key = jnp.sum(held.astype(jnp.int32), axis=0)
    per_key_steps = (per_key + 1) // 2
    start = jnp.sum(jnp.where(key_ids[None, :] < key_ids[:, None], per_key_steps[None, :], 0), axis=1)
    before = (keys[:, None] == keys[None, :]) & (ids[None, :] < ids[:, None])
    rank = jnp.sum(before.astype(jnp.int32), axis=1)
    place = 2 * jnp.sum(jnp.where(held, start[None, :], 0), axis=1) + rank
    spots = jnp.arange(2 * steps, dtype=jnp.int32)
    hit = (place[None, :] == spots[:, None]) & live[None, :]
    tile_at = jnp.min(jnp.where(hit, ids[None, :], tile_cap), axis=1)
    source_at = jnp.max(jnp.where(hit, sources[None, :], 0), axis=1)
    step_ids = jnp.arange(steps, dtype=jnp.int32)
    total = jnp.sum(per_key_steps)
    target = jnp.sum((start[None, :] <= step_ids[:, None]).astype(jnp.int32), axis=1) - 1
    target = jnp.where(step_ids < total, target, key_count)
    first = jnp.max((start[None, :] == step_ids[:, None]).astype(jnp.int32), axis=1)
    first = jnp.where(step_ids < total, first, 1)
    turns = (total + UNROLL - 1) // UNROLL
    return jnp.concatenate([tile_at, source_at, target, first, turns[None]]), steps


def tiles_kernel(table, data, tiles, out, tile_buf, acc, sem, *, steps, transposed):
    tile_cap, tile_len, _ = tiles.shape
    out_count = out.shape[0]
    copy = pltpu.make_async_copy(tiles, tile_buf.at[pl.ds(0, tile_cap)], sem)
    copy.start()
    tile_buf[tile_cap] = jnp.zeros((tile_len, tile_len), tile_buf.dtype)
    copy.wait()

    def turn(index, carry):
        products = []
        for u in range(UNROLL):
            step = index * UNROLL + u
            tile_0 = tile_buf[table[2 * step]]
            tile_1 = tile_buf[table[2 * step + 1]]
            data_0 = data[table[2 * steps + 2 * step]]
            data_1 = data[table[2 * steps + 2 * step + 1]]
            values = jnp.concatenate([data_0, data_1], axis=0)
            if transposed:
                pair = jnp.concatenate([tile_0, tile_1], axis=0)
                dims = (((0,), (0,)), ((), ()))
            else:
                pair = jnp.concatenate([tile_0, tile_1], axis=1)
                dims = (((1,), (0,)), ((), ()))
            products.append(
                lax.dot_general(pair, values, dims, preferred_element_type=jnp.float32)
            )
        for u in range(UNROLL):
            step = index * UNROLL + u
            target = table[4 * steps + step]
            first = table[5 * steps + step]
            acc[target] = jnp.where(first == 1, 0.0, acc[target]) + products[u]
        return carry

    lax.fori_loop(0, table[6 * steps], turn, 0)

    def finish(index, carry):
        out[index] = acc[index].astype(out.dtype)
        return carry

    lax.fori_loop(0, out_count, finish, 0)


def run_tiles(table, steps, data, tiles, out_count, transposed):
    tile_cap, tile_len, _ = tiles.shape
    width = data.shape[2]
    return pl.pallas_call(
        functools.partial(tiles_kernel, steps=steps, transposed=transposed),
        out_shape=jax.ShapeDtypeStruct((out_count, tile_len, width), jnp.bfloat16),
        in_specs=[
            pl.BlockSpec(memory_space=pltpu.SMEM),
            pl.BlockSpec(memory_space=pltpu.VMEM),
            pl.BlockSpec(memory_space=pl.ANY),
        ],
        out_specs=pl.BlockSpec(memory_space=pltpu.VMEM),
        scratch_shapes=[
            pltpu.VMEM((tile_cap + 1, tile_len, tile_len), tiles.dtype),
            pltpu.VMEM((out_count + 1, tile_len, width), jnp.float32),
            pltpu.SemaphoreType.DMA,
        ],
        name="tiles_t" if transposed else "tiles",
    )(table, data, tiles)


def pick_kernel(choice, own, out, sems):
    count = out.shape[0]
    copies = [
        pltpu.make_async_copy(own.at[choice[s]], out.at[s], sems.at[s]) for s in range(count)
    ]
    for copy in copies:
        copy.start()
    for copy in copies:
        copy.wait()


def pick_blocks(choice, own):
    count = choice.shape[0]
    return pl.pallas_call(
        pick_kernel,
        out_shape=jax.ShapeDtypeStruct((count, *own.shape[1:]), own.dtype),
        in_specs=[
            pl.BlockSpec(memory_space=pltpu.SMEM),
            pl.BlockSpec(memory_space=pltpu.VMEM),
        ],
        out_specs=pl.BlockSpec(memory_space=pl.ANY),
        scratch_shapes=[pltpu.SemaphoreType.DMA((count,))],
        name="pick",
    )(choice, own)


def place_kernel(choice, returned, base, extra, out, acc):
    acc[...] = base[...].astype(jnp.float32) + extra[...]

    def add(index, carry):
        block = choice[index]
        acc[block] += returned[index].astype(jnp.float32)
        return carry

    lax.fori_loop(0, returned.shape[0], add, 0, unroll=4)
    out[...] = acc[...].astype(out.dtype)


def place_blocks(choice, returned, base, extra):
    return pl.pallas_call(
        place_kernel,
        out_shape=jax.ShapeDtypeStruct(base.shape, base.dtype),
        in_specs=[
            pl.BlockSpec(memory_space=pltpu.SMEM),
            pl.BlockSpec(memory_space=pltpu.VMEM),
            pl.BlockSpec(memory_space=pltpu.VMEM),
            pl.BlockSpec(memory_space=pltpu.VMEM),
        ],
        out_specs=pl.BlockSpec(memory_space=pltpu.VMEM),
        scratch_shapes=[pltpu.VMEM(base.shape, jnp.float32)],
        name="place",
    )(choice, returned, base, extra)


def reduce_weights(value):
    near = lax.axis_size(NEAR)
    far = lax.axis_size(FAR)
    rows, cols = value.shape
    own_rows = rows // (near * far)
    parts = value.reshape(far, near, own_rows, cols).transpose(1, 0, 2, 3)
    parts = exchange(parts.astype(jnp.bfloat16), NEAR)
    nearer = parts.astype(jnp.float32).sum(axis=0)
    arrived = exchange(nearer.astype(jnp.bfloat16), FAR)
    return arrived.astype(jnp.float32).sum(axis=0)


def body(feats, tile_vals, tile_rows, tile_slots, tile_count, send_list, w_in, w_out, cotangent):
    row_count = lax.axis_size(ROW)
    grp_count = lax.axis_size("grp")
    node_count, width = feats.shape
    tile_len = tile_vals.shape[1]
    per_dev = node_count // tile_len
    slot_count = row_count
    panel_len = grp_count * per_dev
    layer_count = w_in.shape[0]
    count = tile_count[0]
    outgoing = send_list[0].reshape(slot_count)
    row_table, row_steps = pair_table(tile_rows, panel_len, tile_slots, count)
    slot_table, slot_steps = pair_table(tile_slots, slot_count, tile_rows, count)
    factor = float(node_count * lax.axis_size(GRP_ROW)) ** (-0.5)
    contract_rows = (((0,), (0,)), ((), ()))
    contract_cols = (((1,), (1,)), ((), ()))
    hidden = feats
    saved = []
    for layer in range(layer_count):
        own_blocks = hidden.reshape(per_dev, tile_len, width)
        slot_data = exchange(pick_blocks(outgoing, own_blocks), ROW)
        partial_value = run_tiles(row_table, row_steps, slot_data, tile_vals, panel_len, False)
        arrived = exchange(partial_value.reshape(grp_count, node_count, width), "grp")
        message = arrived.astype(jnp.float32).sum(axis=0)
        summed = message + hidden.astype(jnp.float32)
        norm_scale = lax.rsqrt(jnp.mean(summed * summed, axis=-1, keepdims=True) + eps)
        normed = summed * norm_scale
        normed_b = normed.astype(jnp.bfloat16)
        pre_act = jnp.dot(normed_b, w_in[layer], preferred_element_type=jnp.float32)
        activated = jax.nn.silu(pre_act).astype(jnp.bfloat16)
        update = jnp.dot(activated, w_out[layer], preferred_element_type=jnp.float32)
        saved.append((norm_scale, normed, normed_b, pre_act, activated))
        hidden = (hidden.astype(jnp.float32) + update).astype(jnp.bfloat16)
    grad_now = cotangent
    in_sums = [None] * layer_count
    out_sums = [None] * layer_count
    for layer in reversed(range(layer_count)):
        norm_scale, normed, normed_b, pre_act, activated = saved[layer]
        out_term = lax.dot_general(
            activated, grad_now, contract_rows, preferred_element_type=jnp.float32
        )
        d_act = lax.dot_general(
            grad_now, w_out[layer], contract_cols, preferred_element_type=jnp.float32
        )
        sigma = jax.nn.sigmoid(pre_act)
        d_pre = (d_act * sigma * (1.0 + pre_act * (1.0 - sigma))).astype(jnp.bfloat16)
        in_term = lax.dot_general(
            normed_b, d_pre, contract_rows, preferred_element_type=jnp.float32
        )
        in_sums[layer] = reduce_weights(in_term)
        out_sums[layer] = reduce_weights(out_term)
        d_unit = lax.dot_general(
            d_pre, w_in[layer], contract_cols, preferred_element_type=jnp.float32
        )
        d_summed = norm_scale * (
            d_unit - normed * jnp.mean(d_unit * normed, axis=-1, keepdims=True)
        )
        d_summed_b = d_summed.astype(jnp.bfloat16)
        panel_grad = exchange(
            jnp.broadcast_to(d_summed_b[None], (grp_count, node_count, width)), "grp"
        ).reshape(panel_len, tile_len, width)
        per_slot = run_tiles(slot_table, slot_steps, panel_grad, tile_vals, slot_count, True)
        returned = exchange(per_slot, ROW)
        block_dims = (per_dev, tile_len, width)
        grad_now = place_blocks(
            outgoing, returned, grad_now.reshape(block_dims), d_summed.reshape(block_dims)
        ).reshape(node_count, width)
    w_in_grad = jnp.stack(in_sums) * factor
    w_out_grad = jnp.stack(out_sums) * factor
    return (grad_now, w_in_grad, w_out_grad)


def solution(mesh):
    torus = Mesh(
        mesh.devices.reshape(mesh.shape["grp"], 4, 4, 2), ("grp", "row_0", "row_1", "row_2")
    )
    in_specs = (
        P(GRP_ROW, None),
        P(GRP_ROW, None, None),
        P(GRP_ROW),
        P(GRP_ROW),
        P(GRP_ROW),
        P(GRP_ROW, None, None),
        P(),
        P(),
        P(GRP_ROW, None),
    )
    out_specs = (P(GRP_ROW, None), P(None, GRP_ROW, None), P(None, GRP_ROW, None))
    return jax.shard_map(body, mesh=torus, in_specs=in_specs, out_specs=out_specs, check_vma=False)
```

time: 854 us -> 515 us (0.60)
  starting transfers between devices: 225 us -> 70.2 us
  other arithmetic: 125 us -> 21.8 us
  Pallas kernels: 0 us -> 48.3 us
  local copies, waits for them, and re-layouts: 69 us -> 21.6 us
  waiting for transfers between devices: 255 us -> 219 us
  matrix products: 49.3 us -> 20.6 us
  blocking collectives: 114 us -> 104 us
    all_to_all x9 -> x11, starting transfers between devices: 225 us -> 70.2 us  [exchange(): return lax.all_to_all(value, axis, split_axis=0, concat_axis=0, tiled=True)]
    scatter-add x4 -> x0, other arithmetic: 74.7 us -> none  [the longest x2 37.7 us: backward_advance(): return totals.at[slot_ids].add(products * live_mask[:, None, None])]
    pallas_call x0 -> x8, Pallas kernels: none -> 48.3 us  [the longest x4 32.7 us: run_tiles(): pl.pallas_call(functools.partial(tiles_kernel, steps=steps, transposed=tr...]
    dot_general x6 -> x0, matrix products: 37.5 us -> none  [the longest x2 14.2 us: forward_advance(): jnp.einsum('tij,tjd->tid', tile_set, sources, preferred_element_type=jnp....]
    all_to_all x9 -> x11, waiting for transfers between devices: 255 us -> 219 us  [exchange(): return lax.all_to_all(value, axis, split_axis=0, concat_axis=0, tiled=True)]
    gather x6 -> x0, local copies, waits for them, and re-layouts: 21.9 us -> none  [the longest x2 9.88 us: forward_advance(): sources = jnp.take(slot_data, slot_ids, axis=0)]
    reshape x4 -> x0, other arithmetic: 21.1 us -> none  [the longest x2 11.9 us: body(): per_slot.astype(jnp.bfloat16).reshape(row_count, slot_cap, tile_len, width)]
    another operation x6 -> x0, local copies, waits for them, and re-layouts: 19.1 us -> none
  transfers between devices with their start and end apart: 9 -> 11, of which waited for: 7 -> 10; matrix products, arithmetic and copies ran while one was open for 9% -> 9% of each run, Pallas kernels for 0% -> 4%
where the time goes in v1:
time: 515 us; the launch traced here: 508 us
  waiting for transfers between devices  219 us (43%)
  blocking collectives  104 us (20%)
  starting transfers between devices  70.2 us (14%)
  Pallas kernels  48.3 us (9%)
  other arithmetic  21.8 us (4%)
  local copies, waits for them, and re-layouts  21.6 us (4%)
  matrix products  20.6 us (4%)
    all_to_all x11, waiting for transfers between devices, exchange(): return lax.all_to_all(value, axis, split_axis=0, concat_axis=0, tiled=True)  219 us
    all_to_all x5, blocking collectives, exchange(): return lax.all_to_all(value, axis, split_axis=0, concat_axis=0, tiled=True)  104 us
    all_to_all x11, starting transfers between devices, exchange(): return lax.all_to_all(value, axis, split_axis=0, concat_axis=0, tiled=True)  70.2 us
    pallas_call x4, Pallas kernels, run_tiles(): pl.pallas_call(functools.partial(tiles_kernel, steps=steps, transposed=tr...  32.7 us
  transfers between devices with their start and end apart: 11, of which 10 were waited for; matrix products, arithmetic and copies ran while one was open for 9% of the time, Pallas kernels for 4%

profile of v1, /device:TPU:32, one launch (start us, length us, event | category | flops | bytes accessed | tf_op | source)
XLA Modules:
  0.0 508.4 jit_solution(5411115015735192392)
XLA Ops:
  0.6 3.3 pick.2
  4.0 8.1 %all-to-all-start = ((bf16[32,128,512]{2,1,0:T(8,128)(2,1)}), bf16[32,128,512]{2,1,0:T(8,128)(2,1)}, u32[]{:S(2)}, u32[]{:S(2)}) async-start(bf16[32,128,512]{2,1,0:T(8,128)(2,1)} %pick.2), calls=%async_computation | async-start | bytes 8388608 | tf_op jit(solution)/shard_map/all_to_all | solution.py:21
  16.1 47.1 %all-to-all-done.data = bf16[32,128,512]{2,1,0:T(8,128)(2,1)} async-done(((bf16[32,128,512]{2,1,0:T(8,128)(2,1)}), bf16[32,128,512]{2,1,0:T(8,128)(2,1)}, u32[]{:S(2)}, u32[]{:S(2)}) %all-to-all-start) | async-done | bytes 4194336 | tf_op jit(solution)/shard_map/all_to_all | solution.py:21
  63.2 7.6 %tiles.6 = bf16[16,128,512]{2,1,0:T(8,128)(2,1)} custom-call(s32[337]{0:T(512)} %concatenate.7.table, bf16[32,128,512]{2,1,0:T(8,128)(2,1)} %all-to-all-done.data, bf16[96,128,128]{2,1,0:T(8,128)(2,1)} %tiles.11), custom_call_target="tpu_custom_call" | custom-call | tf_op jit(solution)/shard_map/tiles/pallas_call | solution.py:96
  70.8 29.9 %all_to_all.80 = bf16[4,512,512]{2,1,0:T(8,128)(2,1)S(1)} all-to-all(bf16[4,512,512]{2,1,0:T(8,128)(2,1)} %bitcast.91), channel_id=1, replica_groups=mesh['grp'=4,'row_0'=4,'row_1'=4,'row_2'=2] {'grp'}, dimensions={0} | all-to-all | bytes 4194304 | tf_op jit(solution)/shard_map/all_to_all | solution.py:21
  103.3 1.9 fusion.3
  106.8 3.4 pick.3
  110.2 55.7 %all_to_all.81.data = bf16[32,128,512]{2,1,0:T(8,128)(2,1)} all-to-all(bf16[32,128,512]{2,1,0:T(8,128)(2,1)} %pick.3), channel_id=1, replica_groups=mesh['grp'=4,'row_0'=4,'row_1'=4,'row_2'=2] {'row_0','row_1','row_2'}, dimensions={0} | all-to-all | bytes 8388608 | tf_op jit(solution)/shard_map/all_to_all | solution.py:21
  165.8 7.6 %tiles.8 = bf16[16,128,512]{2,1,0:T(8,128)(2,1)} custom-call(s32[337]{0:T(512)} %concatenate.7.table, bf16[32,128,512]{2,1,0:T(8,128)(2,1)} %all_to_all.81.data, bf16[96,128,128]{2,1,0:T(8,128)(2,1)} %tiles.11), custom_call_target="tpu_custom_call" | custom-call | tf_op jit(solution)/shard_map/tiles/pallas_call | solution.py:96
  173.4 4.5 all-to-all-start.3
  178.8 26.7 %all-to-all-done.3 = bf16[4,512,512]{2,1,0:T(8,128)(2,1)} async-done(((bf16[4,512,512]{2,1,0:T(8,128)(2,1)}), bf16[4,512,512]{2,1,0:T(8,128)(2,1)}, u32[]{:S(2)}, u32[]{:S(2)}) %all-to-all-start.3) | async-done | bytes 2097184 | tf_op jit(solution)/shard_map/all_to_all | solution.py:21
  205.6 2.0 convert_reduce_fusion
  216.1 4.4 all-to-all-start.4
  223.1 2.4 convolution_convert_fusion
  227.0 1.7 convolution_convert_fusion.2
  231.6 15.7 %all-to-all-done.4 = bf16[4,512,512]{2,1,0:T(8,128)(2,1)} async-done(((bf16[4,512,512]{2,1,0:T(8,128)(2,1)}), bf16[4,512,512]{2,1,0:T(8,128)(2,1)}, u32[]{:S(2)}, u32[]{:S(2)}) %all-to-all-start.4) | async-done | bytes 2097184 | tf_op jit(solution)/shard_map/all_to_all | solution.py:21
  247.3 3.6 all-to-all-start.14
  250.9 8.8 %tiles_t.2 = bf16[32,128,512]{2,1,0:T(8,128)(2,1)} custom-call(s32[385]{0:T(512)} %concatenate.6.table, bf16[16,128,512]{2,1,0:T(8,128)(2,1)} %bitcast.12.data, bf16[96,128,128]{2,1,0:T(8,128)(2,1)} %tiles.11), custom_call_target="tpu_custom_call" | custom-call | tf_op jit(solution)/shard_map/tiles_t/pallas_call | solution.py:96
  259.7 6.9 %all_to_all.82 = bf16[2,64,4,1024]{3,2,1,0:T(4,128)(2,1)} all-to-all(bf16[2,64,4,1024]{3,2,1,0:T(4,128)(2,1)} %bitcast.95), channel_id=1, replica_groups=mesh['grp'=4,'row_0'=4,'row_1'=4,'row_2'=2] {'row_2'}, dimensions={0} | all-to-all | bytes 2097152 | tf_op jit(solution)/shard_map/all_to_all | solution.py:21
  266.6 6.8 %all-to-all-start.5 = ((bf16[32,128,512]{2,1,0:T(8,128)(2,1)}), bf16[32,128,512]{2,1,0:T(8,128)(2,1)}, u32[]{:S(2)}, u32[]{:S(2)}) async-start(bf16[32,128,512]{2,1,0:T(8,128)(2,1)} %tiles_t.2), calls=%async_computation.5 | async-start | bytes 8388608 | tf_op jit(solution)/shard_map/all_to_all | solution.py:21
  273.5 2.3 copy.35
  276.9 2.9 reduce_sum.266
  279.7 44.8 %all-to-all-done.5.returned = bf16[32,128,512]{2,1,0:T(8,128)(2,1)} async-done(((bf16[32,128,512]{2,1,0:T(8,128)(2,1)}), bf16[32,128,512]{2,1,0:T(8,128)(2,1)}, u32[]{:S(2)}, u32[]{:S(2)}) %all-to-all-start.5) | async-done | bytes 4194336 | tf_op jit(solution)/shard_map/all_to_all | solution.py:21
  324.6 8.0 %all-to-all-start.15 = ((bf16[64,8,512]{2,1,0:T(8,128)(2,1)}), bf16[64,8,512]{2,1,0:T(8,128)(2,1)}, u32[]{:S(2)}, u32[]{:S(2)}) async-start(bf16[64,8,512]{2,1,0:T(8,128)(2,1)} %reduce_sum.270), calls=%async_computation.15 | async-start | bytes 1048576 | tf_op jit(solution)/shard_map/all_to_all | solution.py:21
  332.6 4.5 place.2.base
  337.1 1.9 fusion.4
  340.1 2.1 multiply_convert_fusion.1
  342.2 1.7 all-to-all-done.15
  343.9 5.7 %all_to_all.83 = bf16[2,64,8,512]{3,2,1,0:T(8,128)(2,1)S(1)} all-to-all(bf16[2,64,8,512]{3,2,1,0:T(8,128)(2,1)} %copy.36), channel_id=1, replica_groups=mesh['grp'=4,'row_0'=4,'row_1'=4,'row_2'=2] {'row_2'}, dimensions={0} | all-to-all | bytes 2097152 | tf_op jit(solution)/shard_map/all_to_all | solution.py:21
  349.6 8.7 %all-to-all-start.11 = ((bf16[64,4,1024]{2,1,0:T(4,128)(2,1)}), bf16[64,4,1024]{2,1,0:T(4,128)(2,1)S(1)}, u32[]{:S(2)}, u32[]{:S(2)}) async-start(bf16[64,4,1024]{2,1,0:T(4,128)(2,1)} %reduce_sum.266), calls=%async_computation.11 | async-start | bytes 1048576 | tf_op jit(solution)/shard_map/all_to_all | solution.py:21
  358.3 3.1 convolution_convert_fusion.3
  361.4 2.3 convert_element_type.141
  363.6 2.5 copy.46
  367.3 3.4 multiply_reduce_fusion
  371.0 5.4 %all_to_all.84 = bf16[2,64,4,1024]{3,2,1,0:T(4,128)(2,1)} all-to-all(bf16[2,64,4,1024]{3,2,1,0:T(4,128)(2,1)S(1)} %bitcast.96), channel_id=1, replica_groups=mesh['grp'=4,'row_0'=4,'row_1'=4,'row_2'=2] {'row_2'}, dimensions={0} | all-to-all | bytes 2097152 | tf_op jit(solution)/shard_map/all_to_all | solution.py:21
  376.3 10.1 %all-to-all-start.13 = ((bf16[64,8,512]{2,1,0:T(8,128)(2,1)}), bf16[64,8,512]{2,1,0:T(8,128)(2,1)S(1)}, u32[]{:S(2)}, u32[]{:S(2)}) async-start(bf16[64,8,512]{2,1,0:T(8,128)(2,1)} %reduce_sum.268), calls=%async_computation.13 | async-start | bytes 1048576 | tf_op jit(solution)/shard_map/all_to_all | solution.py:21
  386.4 2.5 fusion.32
  388.9 10.2 %all-to-all-done.13 = bf16[64,8,512]{2,1,0:T(8,128)(2,1)S(1)} async-done(((bf16[64,8,512]{2,1,0:T(8,128)(2,1)}), bf16[64,8,512]{2,1,0:T(8,128)(2,1)S(1)}, u32[]{:S(2)}, u32[]{:S(2)}) %all-to-all-start.13) | async-done | bytes 524320 | tf_op jit(solution)/shard_map/all_to_all | solution.py:21
  399.1 1.5 broadcast_in_dim.181
  400.7 3.7 all-to-all-start.6
  404.4 1.9 reduce_sum.264
  406.3 23.5 %all-to-all-done.6 = bf16[4,512,512]{2,1,0:T(8,128)(2,1)S(1)} async-done(((bf16[4,512,512]{2,1,0:T(8,128)(2,1)}), bf16[4,512,512]{2,1,0:T(8,128)(2,1)S(1)}, u32[]{:S(2)}, u32[]{:S(2)}) %all-to-all-start.6) | async-done | bytes 2097184 | tf_op jit(solution)/shard_map/all_to_all | solution.py:21
  429.8 6.2 %all-to-all-start.9 = ((bf16[64,4,1024]{2,1,0:T(4,128)(2,1)}), bf16[64,4,1024]{2,1,0:T(4,128)(2,1)}, u32[]{:S(2)}, u32[]{:S(2)}) async-start(bf16[64,4,1024]{2,1,0:T(4,128)(2,1)} %reduce_sum.264), calls=%async_computation.9 | async-start | bytes 1048576 | tf_op jit(solution)/shard_map/all_to_all | solution.py:21
  436.1 8.8 %tiles_t.3 = bf16[32,128,512]{2,1,0:T(8,128)(2,1)} custom-call(s32[385]{0:T(512)} %concatenate.6.table, bf16[16,128,512]{2,1,0:T(8,128)(2,1)} %bitcast.89, bf16[96,128,128]{2,1,0:T(8,128)(2,1)} %tiles.11), custom_call_target="tpu_custom_call" | custom-call | tf_op jit(solution)/shard_map/tiles_t/pallas_call | solution.py:96
  444.9 2.2 all-to-all-done.9
  447.1 6.0 %all-to-all-start.7 = ((bf16[32,128,512]{2,1,0:T(8,128)(2,1)}), bf16[32,128,512]{2,1,0:T(8,128)(2,1)}, u32[]{:S(2)}, u32[]{:S(2)}) async-start(bf16[32,128,512]{2,1,0:T(8,128)(2,1)} %tiles_t.3), calls=%async_computation.7 | async-start | bytes 8388608 | tf_op jit(solution)/shard_map/all_to_all | solution.py:21
  457.0 47.0 %all-to-all-done.7.returned = bf16[32,128,512]{2,1,0:T(8,128)(2,1)} async-done(((bf16[32,128,512]{2,1,0:T(8,128)(2,1)}), bf16[32,128,512]{2,1,0:T(8,128)(2,1)}, u32[]{:S(2)}, u32[]{:S(2)}) %all-to-all-start.7) | async-done | bytes 4194336 | tf_op jit(solution)/shard_map/all_to_all | solution.py:21
  504.0 4.4 place.3
  (100 shorter events, 30.0 us)
Async XLA Ops:
  3.9 8.8 %copy-start.17 = (s32[96]{0:T(128)S(1)}, s32[96]{0:T(128)}, u32[]{:S(2)}) copy-start(s32[96]{0:T(128)} %param.11) | copy-start | bytes 1156
  4.0 10.7 %copy-start.16 = (s32[96]{0:T(128)S(1)}, s32[96]{0:T(128)}, u32[]{:S(2)}) copy-start(s32[96]{0:T(128)} %param.12) | copy-start | bytes 1156
  4.0 59.2 %all-to-all-start = ((bf16[32,128,512]{2,1,0:T(8,128)(2,1)}), bf16[32,128,512]{2,1,0:T(8,128)(2,1)}, u32[]{:S(2)}, u32[]{:S(2)}) async-start(bf16[32,128,512]{2,1,0:T(8,128)(2,1)} %pick.2), calls=%async_computation | async-start | bytes 8388608 | tf_op jit(solution)/shard_map/all_to_all | solution.py:21
  100.6 1.0 copy-start
  101.7 1.6 copy-start.12
  103.3 2.0 copy-start.15
  103.3 2.0 copy-start.18
  105.2 1.5 copy-start.23
  173.4 32.1 %all-to-all-start.3 = ((bf16[4,512,512]{2,1,0:T(8,128)(2,1)}), bf16[4,512,512]{2,1,0:T(8,128)(2,1)}, u32[]{:S(2)}, u32[]{:S(2)}) async-start(bf16[4,512,512]{2,1,0:T(8,128)(2,1)} %bitcast.90), calls=%async_computation.3 | async-start | bytes 4194304 | tf_op jit(solution)/shard_map/all_to_all | solution.py:21
  177.9 29.6 %copy-start.1 = (bf16[512,512]{1,0:T(8,128)(2,1)S(1)}, bf16[512,512]{1,0:T(8,128)(2,1)}, u32[]{:S(2)}) copy-start(bf16[512,512]{1,0:T(8,128)(2,1)} %fusion.5) | copy-start | bytes 1572868
  207.6 1.6 copy-start.13
  209.2 1.0 copy-start.14
  209.2 1.8 copy-start.19
  210.9 1.4 copy-start.6
  212.4 1.0 copy-start.21
  216.1 31.2 %all-to-all-start.4 = ((bf16[4,512,512]{2,1,0:T(8,128)(2,1)}), bf16[4,512,512]{2,1,0:T(8,128)(2,1)}, u32[]{:S(2)}, u32[]{:S(2)}) async-start(bf16[4,512,512]{2,1,0:T(8,128)(2,1)} %broadcast_in_dim.180), calls=%async_computation.4 | async-start | bytes 4194304 | tf_op jit(solution)/shard_map/all_to_all | solution.py:21
  225.4 1.6 copy-start.22
  247.3 12.4 %all-to-all-start.14 = ((bf16[2,64,8,512]{3,2,1,0:T(8,128)(2,1)}), bf16[2,64,8,512]{3,2,1,0:T(8,128)(2,1)S(1)}, u32[]{:S(2)}, u32[]{:S(2)}) async-start(bf16[2,64,8,512]{3,2,1,0:T(8,128)(2,1)} %bitcast.94), calls=%async_computation.14 | async-start | bytes 2097152 | tf_op jit(solution)/shard_map/all_to_all | solution.py:21
  266.6 57.9 %all-to-all-start.5 = ((bf16[32,128,512]{2,1,0:T(8,128)(2,1)}), bf16[32,128,512]{2,1,0:T(8,128)(2,1)}, u32[]{:S(2)}, u32[]{:S(2)}) async-start(bf16[32,128,512]{2,1,0:T(8,128)(2,1)} %tiles_t.2), calls=%async_computation.5 | async-start | bytes 8388608 | tf_op jit(solution)/shard_map/all_to_all | solution.py:21
  324.6 19.3 %all-to-all-start.15 = ((bf16[64,8,512]{2,1,0:T(8,128)(2,1)}), bf16[64,8,512]{2,1,0:T(8,128)(2,1)}, u32[]{:S(2)}, u32[]{:S(2)}) async-start(bf16[64,8,512]{2,1,0:T(8,128)(2,1)} %reduce_sum.270), calls=%async_computation.15 | async-start | bytes 1048576 | tf_op jit(solution)/shard_map/all_to_all | solution.py:21
  332.6 4.5 copy-start.11
  337.1 3.0 copy-start.5
  337.1 3.0 copy-start.20
  337.1 3.0 copy-start.24
  349.6 21.4 %all-to-all-start.11 = ((bf16[64,4,1024]{2,1,0:T(4,128)(2,1)}), bf16[64,4,1024]{2,1,0:T(4,128)(2,1)S(1)}, u32[]{:S(2)}, u32[]{:S(2)}) async-start(bf16[64,4,1024]{2,1,0:T(4,128)(2,1)} %reduce_sum.266), calls=%async_computation.11 | async-start | bytes 1048576 | tf_op jit(solution)/shard_map/all_to_all | solution.py:21
  367.3 3.7 copy-start.4
  371.0 18.0 %copy-start.7 = (bf16[64,4,1024]{2,1,0:T(4,128)(2,1)}, bf16[64,4,1024]{2,1,0:T(4,128)(2,1)S(1)}, u32[]{:S(2)}) copy-start(bf16[64,4,1024]{2,1,0:T(4,128)(2,1)S(1)} %all-to-all-done.11) | copy-start | bytes 1572868
  376.3 22.8 %all-to-all-start.13 = ((bf16[64,8,512]{2,1,0:T(8,128)(2,1)}), bf16[64,8,512]{2,1,0:T(8,128)(2,1)S(1)}, u32[]{:S(2)}, u32[]{:S(2)}) async-start(bf16[64,8,512]{2,1,0:T(8,128)(2,1)} %reduce_sum.268), calls=%async_computation.13 | async-start | bytes 1048576 | tf_op jit(solution)/shard_map/all_to_all | solution.py:21
  399.1 1.5 copy-start.9
  400.7 3.8 copy-start.3
  400.7 29.2 %all-to-all-start.6 = ((bf16[4,512,512]{2,1,0:T(8,128)(2,1)}), bf16[4,512,512]{2,1,0:T(8,128)(2,1)S(1)}, u32[]{:S(2)}, u32[]{:S(2)}) async-start(bf16[4,512,512]{2,1,0:T(8,128)(2,1)} %broadcast_in_dim.181), calls=%async_computation.6 | async-start | bytes 4194304 | tf_op jit(solution)/shard_map/all_to_all | solution.py:21
  429.8 6.3 %copy-start.2 = (bf16[4,512,512]{2,1,0:T(8,128)(2,1)}, bf16[4,512,512]{2,1,0:T(8,128)(2,1)S(1)}, u32[]{:S(2)}) copy-start(bf16[4,512,512]{2,1,0:T(8,128)(2,1)S(1)} %all-to-all-done.6) | copy-start | bytes 6291460
  429.8 17.3 %all-to-all-start.9 = ((bf16[64,4,1024]{2,1,0:T(4,128)(2,1)}), bf16[64,4,1024]{2,1,0:T(4,128)(2,1)}, u32[]{:S(2)}, u32[]{:S(2)}) async-start(bf16[64,4,1024]{2,1,0:T(4,128)(2,1)} %reduce_sum.264), calls=%async_computation.9 | async-start | bytes 1048576 | tf_op jit(solution)/shard_map/all_to_all | solution.py:21
  444.9 9.3 %copy-start.8 = (bf16[64,4,1024]{2,1,0:T(4,128)(2,1)S(1)}, bf16[64,4,1024]{2,1,0:T(4,128)(2,1)}, u32[]{:S(2)}) copy-start(bf16[64,4,1024]{2,1,0:T(4,128)(2,1)} %copy-done.7) | copy-start | bytes 1572868
  444.9 9.5 %copy-start.10 = (bf16[64,8,512]{2,1,0:T(8,128)(2,1)S(1)}, bf16[64,8,512]{2,1,0:T(8,128)(2,1)}, u32[]{:S(2)}) copy-start(bf16[64,8,512]{2,1,0:T(8,128)(2,1)} %copy-done.9) | copy-start | bytes 1572868
  447.1 56.9 %all-to-all-start.7 = ((bf16[32,128,512]{2,1,0:T(8,128)(2,1)}), bf16[32,128,512]{2,1,0:T(8,128)(2,1)}, u32[]{:S(2)}, u32[]{:S(2)}) async-start(bf16[32,128,512]{2,1,0:T(8,128)(2,1)} %tiles_t.3), calls=%async_computation.7 | async-start | bytes 8388608 | tf_op jit(solution)/shard_map/all_to_all | solution.py:21

commit v2 on v1

--- a/solution.py
+++ b/solution.py
@@ -15,6 +15,7 @@
 
 eps = 1e-06
 UNROLL = 4
+CHUNKS = 2
 
 
 def exchange(value, axis):
@@ -48,13 +49,26 @@
     return jnp.concatenate([tile_at, source_at, target, first, turns[None]]), steps
 
 
-def tiles_kernel(table, data, tiles, out, tile_buf, acc, sem, *, steps, transposed):
+def tiles_kernel(table, *refs, steps, transposed, piece_count, out_pieces):
+    data_pieces = refs[:piece_count]
+    tiles = refs[piece_count]
+    outs = refs[piece_count + 1 : piece_count + 1 + out_pieces]
+    data, tile_buf, acc, data_sems, tile_sem = refs[piece_count + 1 + out_pieces :]
     tile_cap, tile_len, _ = tiles.shape
-    out_count = out.shape[0]
-    copy = pltpu.make_async_copy(tiles, tile_buf.at[pl.ds(0, tile_cap)], sem)
-    copy.start()
+    piece_len = data_pieces[0].shape[0]
+    out_len = outs[0].shape[0]
+    copies = [
+        pltpu.make_async_copy(
+            data_pieces[i], data.at[pl.ds(i * piece_len, piece_len)], data_sems.at[i]
+        )
+        for i in range(piece_count)
+    ]
+    copies.append(pltpu.make_async_copy(tiles, tile_buf.at[pl.ds(0, tile_cap)], tile_sem))
+    for copy in copies:
+        copy.start()
     tile_buf[tile_cap] = jnp.zeros((tile_len, tile_len), tile_buf.dtype)
-    copy.wait()
+    for copy in copies:
+        copy.wait()
 
     def turn(index, carry):
         products = []
@@ -83,32 +97,40 @@
 
     lax.fori_loop(0, table[6 * steps], turn, 0)
 
-    def finish(index, carry):
-        out[index] = acc[index].astype(out.dtype)
-        return carry
-
-    lax.fori_loop(0, out_count, finish, 0)
-
-
-def run_tiles(table, steps, data, tiles, out_count, transposed):
+    for piece in range(out_pieces):
+
+        def finish(index, carry, piece=piece):
+            outs[piece][index] = acc[piece * out_len + index].astype(outs[piece].dtype)
+            return carry
+
+        lax.fori_loop(0, out_len, finish, 0, unroll=2)
+
+
+def run_tiles(table, steps, pieces, tiles, out_count, out_pieces, transposed):
     tile_cap, tile_len, _ = tiles.shape
-    width = data.shape[2]
+    piece_len, _, width = pieces[0].shape
+    out_len = out_count // out_pieces
     return pl.pallas_call(
-        functools.partial(tiles_kernel, steps=steps, transposed=transposed),
-        out_shape=jax.ShapeDtypeStruct((out_count, tile_len, width), jnp.bfloat16),
-        in_specs=[
-            pl.BlockSpec(memory_space=pltpu.SMEM),
-            pl.BlockSpec(memory_space=pltpu.VMEM),
-            pl.BlockSpec(memory_space=pl.ANY),
-        ],
-        out_specs=pl.BlockSpec(memory_space=pltpu.VMEM),
+        functools.partial(
+            tiles_kernel,
+            steps=steps,
+            transposed=transposed,
+            piece_count=len(pieces),
+            out_pieces=out_pieces,
+        ),
+        out_shape=[jax.ShapeDtypeStruct((out_len, tile_len, width), jnp.bfloat16)] * out_pieces,
+        in_specs=[pl.BlockSpec(memory_space=pltpu.SMEM)]
+        + [pl.BlockSpec(memory_space=pl.ANY)] * (len(pieces) + 1),
+        out_specs=[pl.BlockSpec(memory_space=pltpu.VMEM)] * out_pieces,
         scratch_shapes=[
+            pltpu.VMEM((piece_len * len(pieces), tile_len, width), jnp.bfloat16),
             pltpu.VMEM((tile_cap + 1, tile_len, tile_len), tiles.dtype),
             pltpu.VMEM((out_count + 1, tile_len, width), jnp.float32),
+            pltpu.SemaphoreType.DMA((len(pieces),)),
             pltpu.SemaphoreType.DMA,
         ],
         name="tiles_t" if transposed else "tiles",
-    )(table, data, tiles)
+    )(table, *pieces, tiles)
 
 
 def pick_kernel(choice, own, out, sems):
@@ -122,14 +144,16 @@
         copy.wait()
 
 
-def pick_blocks(choice, own):
+def pick_blocks(choice, own, chunk, width):
     count = choice.shape[0]
+    blocks, tile_len, _ = own.shape
     return pl.pallas_call(
         pick_kernel,
-        out_shape=jax.ShapeDtypeStruct((count, *own.shape[1:]), own.dtype),
+        grid=(1,),
+        out_shape=jax.ShapeDtypeStruct((count, tile_len, width), own.dtype),
         in_specs=[
             pl.BlockSpec(memory_space=pltpu.SMEM),
-            pl.BlockSpec(memory_space=pltpu.VMEM),
+            pl.BlockSpec((blocks, tile_len, width), lambda i: (0, 0, chunk)),
         ],
         out_specs=pl.BlockSpec(memory_space=pl.ANY),
         scratch_shapes=[pltpu.SemaphoreType.DMA((count,))],
@@ -149,32 +173,48 @@
     out[...] = acc[...].astype(out.dtype)
 
 
-def place_blocks(choice, returned, base, extra):
+def place_blocks(choice, returned, base, extra, chunk):
+    count, tile_len, width = returned.shape
+    block = (base.shape[0], tile_len, width)
     return pl.pallas_call(
         place_kernel,
-        out_shape=jax.ShapeDtypeStruct(base.shape, base.dtype),
+        grid=(1,),
+        out_shape=jax.ShapeDtypeStruct(block, base.dtype),
         in_specs=[
             pl.BlockSpec(memory_space=pltpu.SMEM),
-            pl.BlockSpec(memory_space=pltpu.VMEM),
-            pl.BlockSpec(memory_space=pltpu.VMEM),
-            pl.BlockSpec(memory_space=pltpu.VMEM),
+            pl.BlockSpec((count, tile_len, width), lambda i: (0, 0, 0)),
+            pl.BlockSpec(block, lambda i: (0, 0, chunk)),
+            pl.BlockSpec(block, lambda i: (0, 0, chunk)),
         ],
-        out_specs=pl.BlockSpec(memory_space=pltpu.VMEM),
-        scratch_shapes=[pltpu.VMEM(base.shape, jnp.float32)],
+        out_specs=pl.BlockSpec(block, lambda i: (0, 0, 0)),
+        scratch_shapes=[pltpu.VMEM(block, jnp.float32)],
         name="place",
     )(choice, returned, base, extra)
 
 
-def reduce_weights(value):
+def shifted(value, axis, step):
+    length = lax.axis_size(axis)
+    return lax.ppermute(value, axis, [(i, (i + step) % length) for i in range(length)])
+
+
+def reduce_weights(in_term, out_term):
     near = lax.axis_size(NEAR)
     far = lax.axis_size(FAR)
-    rows, cols = value.shape
-    own_rows = rows // (near * far)
-    parts = value.reshape(far, near, own_rows, cols).transpose(1, 0, 2, 3)
-    parts = exchange(parts.astype(jnp.bfloat16), NEAR)
+    devices = near * far
+    lanes = 128
+    flat = [
+        term.astype(jnp.bfloat16).reshape(far, near, -1, lanes) for term in (in_term, out_term)
+    ]
+    parts = jnp.concatenate(flat, axis=2).transpose(1, 0, 2, 3)
+    parts = exchange(parts, NEAR)
     nearer = parts.astype(jnp.float32).sum(axis=0)
     arrived = exchange(nearer.astype(jnp.bfloat16), FAR)
-    return arrived.astype(jnp.float32).sum(axis=0)
+    total = arrived.astype(jnp.float32).sum(axis=0)
+    split = in_term.size // devices // lanes
+    return (
+        total[:split].reshape(in_term.shape[0] // devices, in_term.shape[1]),
+        total[split:].reshape(out_term.shape[0] // devices, out_term.shape[1]),
+    )
 
 
 def body(feats, tile_vals, tile_rows, tile_slots, tile_count, send_list, w_in, w_out, cotangent):
@@ -188,8 +228,11 @@
     layer_count = w_in.shape[0]
     count = tile_count[0]
     outgoing = send_list[0].reshape(slot_count)
-    row_table, row_steps = pair_table(tile_rows, panel_len, tile_slots, count)
-    slot_table, slot_steps = pair_table(tile_slots, slot_count, tile_rows, count)
+    chunk_width = width // CHUNKS
+    grp_id = lax.axis_index("grp")
+    near_rows = (tile_rows // per_dev - grp_id) % grp_count * per_dev + tile_rows % per_dev
+    row_table, row_steps = pair_table(near_rows, panel_len, tile_slots, count)
+    slot_table, slot_steps = pair_table(tile_slots, slot_count, near_rows, count)
     factor = float(node_count * lax.axis_size(GRP_ROW)) ** (-0.5)
     contract_rows = (((0,), (0,)), ((), ()))
     contract_cols = (((1,), (1,)), ((), ()))
@@ -197,10 +240,17 @@
     saved = []
     for layer in range(layer_count):
         own_blocks = hidden.reshape(per_dev, tile_len, width)
-        slot_data = exchange(pick_blocks(outgoing, own_blocks), ROW)
-        partial_value = run_tiles(row_table, row_steps, slot_data, tile_vals, panel_len, False)
-        arrived = exchange(partial_value.reshape(grp_count, node_count, width), "grp")
-        message = arrived.astype(jnp.float32).sum(axis=0)
+        messages = []
+        for chunk in range(CHUNKS):
+            slot_data = exchange(pick_blocks(outgoing, own_blocks, chunk, chunk_width), ROW)
+            pieces = run_tiles(
+                row_table, row_steps, [slot_data], tile_vals, panel_len, grp_count, False
+            )
+            total = pieces[0].astype(jnp.float32)
+            for step in (2, 1, 3):
+                total = total + shifted(pieces[step], "grp", step).astype(jnp.float32)
+            messages.append(total.reshape(node_count, chunk_width))
+        message = jnp.concatenate(messages, axis=1)
         summed = message + hidden.astype(jnp.float32)
         norm_scale = lax.rsqrt(jnp.mean(summed * summed, axis=-1, keepdims=True) + eps)
         normed = summed * norm_scale
@@ -226,8 +276,7 @@
         in_term = lax.dot_general(
             normed_b, d_pre, contract_rows, preferred_element_type=jnp.float32
         )
-        in_sums[layer] = reduce_weights(in_term)
-        out_sums[layer] = reduce_weights(out_term)
+        in_sums[layer], out_sums[layer] = reduce_weights(in_term, out_term)
         d_unit = lax.dot_general(
             d_pre, w_in[layer], contract_cols, preferred_element_type=jnp.float32
         )
@@ -235,15 +284,18 @@
             d_unit - normed * jnp.mean(d_unit * normed, axis=-1, keepdims=True)
         )
         d_summed_b = d_summed.astype(jnp.bfloat16)
-        panel_grad = exchange(
-            jnp.broadcast_to(d_summed_b[None], (grp_count, node_count, width)), "grp"
-        ).reshape(panel_len, tile_len, width)
-        per_slot = run_tiles(slot_table, slot_steps, panel_grad, tile_vals, slot_count, True)
-        returned = exchange(per_slot, ROW)
         block_dims = (per_dev, tile_len, width)
-        grad_now = place_blocks(
-            outgoing, returned, grad_now.reshape(block_dims), d_summed.reshape(block_dims)
-        ).reshape(node_count, width)
+        grad_blocks = grad_now.reshape(block_dims)
+        d_blocks = d_summed.reshape(block_dims)
+        d_blocks_b = d_summed_b.reshape(block_dims)
+        updated = []
+        for chunk in range(CHUNKS):
+            own = d_blocks_b[:, :, chunk * chunk_width : (chunk + 1) * chunk_width]
+            pieces = [own] + [shifted(own, "grp", grp_count - step) for step in range(1, grp_count)]
+            per_slot = run_tiles(slot_table, slot_steps, pieces, tile_vals, slot_count, 1, True)[0]
+            returned = exchange(per_slot, ROW)
+            updated.append(place_blocks(outgoing, returned, grad_blocks, d_blocks, chunk))
+        grad_now = jnp.concatenate(updated, axis=2).reshape(node_count, width)
     w_in_grad = jnp.stack(in_sums) * factor
     w_out_grad = jnp.stack(out_sums) * factor
     return (grad_now, w_in_grad, w_out_grad)

time: 515 us -> 467 us (0.907)
  blocking collectives: 104 us -> 6.47 us
  starting transfers between devices: 70.2 us -> 121 us
  waiting for transfers between devices: 219 us -> 188 us
  Pallas kernels: 48.3 us -> 74.3 us
  other arithmetic: 21.8 us -> 28 us
    all_to_all x5 -> x1, blocking collectives: 104 us -> 6.47 us  [exchange(): return lax.all_to_all(value, axis, split_axis=0, concat_axis=0, tiled=True)]
    all_to_all x11, waiting for transfers between devices: 219 us -> 128 us  [exchange(): return lax.all_to_all(value, axis, split_axis=0, concat_axis=0, tiled=True)]
    ppermute x0 -> x24, waiting for transfers between devices: none -> 60.5 us  [shifted(): lax.ppermute(value, axis, [(i, (i + step) % length) for i in range(length)])]
    ppermute x0 -> x24, starting transfers between devices: none -> 42.7 us  [shifted(): lax.ppermute(value, axis, [(i, (i + step) % length) for i in range(length)])]
    pallas_call x4 -> x8, Pallas kernels: 32.7 us -> 52.2 us  [run_tiles(): pl.pallas_call(functools.partial(tiles_kernel, steps=steps, transposed=tr...]
    convert_element_type x7 -> x0, local copies, waits for them, and re-layouts: 12 us -> none  [the longest x6 9.74 us: reduce_weights(): parts = exchange(parts.astype(jnp.bfloat16), NEAR)]
    all_to_all x11, starting transfers between devices: 70.2 us -> 78.3 us  [exchange(): return lax.all_to_all(value, axis, split_axis=0, concat_axis=0, tiled=True)]
    reshape x0 -> x4, local copies, waits for them, and re-layouts: none -> 7.99 us  [reduce_weights(): term.astype(jnp.bfloat16).reshape(far, near, -1, lanes)]
  transfers between devices with their start and end apart: 11 -> 35, of which waited for: 10 -> 21; matrix products, arithmetic and copies ran while one was open for 9% -> 7% of each run, Pallas kernels for 4% -> 14%
where the time goes in v2:
time: 467 us; the launch traced here: 460 us
  waiting for transfers between devices  188 us (40%)
  starting transfers between devices  121 us (26%)
  Pallas kernels  74.3 us (16%)
  other arithmetic  28 us (6%)
  matrix products  20.9 us (4%)
  local copies, waits for them, and re-layouts  17.3 us (4%)
  blocking collectives  6.47 us (1%)
    all_to_all x11, waiting for transfers between devices, exchange(): return lax.all_to_all(value, axis, split_axis=0, concat_axis=0, tiled=True)  128 us
    all_to_all x11, starting transfers between devices, exchange(): return lax.all_to_all(value, axis, split_axis=0, concat_axis=0, tiled=True)  78.3 us
    ppermute x24, waiting for transfers between devices, shifted(): lax.ppermute(value, axis, [(i, (i + step) % length) for i in range(length)])  60.5 us
    pallas_call x8, Pallas kernels, run_tiles(): pl.pallas_call(functools.partial(tiles_kernel, steps=steps, transposed=tr...  52.2 us
    ppermute x24, starting transfers between devices, shifted(): lax.ppermute(value, axis, [(i, (i + step) % length) for i in range(length)])  42.7 us
    pallas_call x4, Pallas kernels, place_blocks(): pl.pallas_call(place_kernel, grid=(1,), out_shape=jax.ShapeDtypeStruct(bl...  11.7 us
    pallas_call x4, Pallas kernels, pick_blocks(): pl.pallas_call(pick_kernel, grid=(1,), out_shape=jax.ShapeDtypeStruct((co...  10.3 us
  transfers between devices with their start and end apart: 35, of which 21 were waited for; matrix products, arithmetic and copies ran while one was open for 7% of the time, Pallas kernels for 14%

profile of v2, /device:TPU:32, one launch (start us, length us, event | category | flops | bytes accessed | tf_op | source)
XLA Modules:
  0.0 459.6 jit_solution(12074849614062987023)
XLA Ops:
  3.2 8.1 %all-to-all-start.1 = ((bf16[32,128,256]{2,1,0:T(8,128)(2,1)}), bf16[32,128,256]{2,1,0:T(8,128)(2,1)S(1)}, u32[]{:S(2)}, u32[]{:S(2)}) async-start(bf16[32,128,256]{2,1,0:T(8,128)(2,1)} %pick.5), calls=%async_computation.1 | async-start | bytes 4194304 | tf_op jit(solution)/shard_map/all_to_all | solution.py:22
  15.7 22.2 %all-to-all-done.1.refs_0_ = bf16[32,128,256]{2,1,0:T(8,128)(2,1)S(1)} async-done(((bf16[32,128,256]{2,1,0:T(8,128)(2,1)}), bf16[32,128,256]{2,1,0:T(8,128)(2,1)S(1)}, u32[]{:S(2)}, u32[]{:S(2)}) %all-to-all-start.1) | async-done | bytes 2097184 | tf_op jit(solution)/shard_map/all_to_all | solution.py:22
  37.9 8.1 %all-to-all-start = ((bf16[32,128,256]{2,1,0:T(8,128)(2,1)}), bf16[32,128,256]{2,1,0:T(8,128)(2,1)}, u32[]{:S(2)}, u32[]{:S(2)}) async-start(bf16[32,128,256]{2,1,0:T(8,128)(2,1)} %pick.4), calls=%async_computation | async-start | bytes 4194304 | tf_op jit(solution)/shard_map/all_to_all | solution.py:22
  50.1 6.1 %tiles.5 = (bf16[4,128,256]{2,1,0:T(8,128)(2,1)}, bf16[4,128,256]{2,1,0:T(8,128)(2,1)}, bf16[4,128,256]{2,1,0:T(8,128)(2,1)}, bf16[4,128,256]{2,1,0:T(8,128)(2,1)}) custom-call(s32[337]{0:T(512)} %concatenate.25.table, bf16[32,128,256]{2,1,0:T(8,128)(2,1)} %copy-done.2, bf16[96,128,128]{2,1,0:T(8,128)(2,1)} %refs_4_.7), custom_call_target="tpu_custom_call" | custom-call | tf_op jit(solution)/shard_map/tiles/pallas_call | solution.py:113
  56.2 3.3 collective-permute-start.3
  62.7 10.0 %all-to-all-done.refs_0_ = bf16[32,128,256]{2,1,0:T(8,128)(2,1)} async-done(((bf16[32,128,256]{2,1,0:T(8,128)(2,1)}), bf16[32,128,256]{2,1,0:T(8,128)(2,1)}, u32[]{:S(2)}, u32[]{:S(2)}) %all-to-all-start) | async-done | bytes 2097184 | tf_op jit(solution)/shard_map/all_to_all | solution.py:22
  72.7 6.1 %tiles.4 = (bf16[4,128,256]{2,1,0:T(8,128)(2,1)}, bf16[4,128,256]{2,1,0:T(8,128)(2,1)}, bf16[4,128,256]{2,1,0:T(8,128)(2,1)}, bf16[4,128,256]{2,1,0:T(8,128)(2,1)}) custom-call(s32[337]{0:T(512)} %concatenate.25.table, bf16[32,128,256]{2,1,0:T(8,128)(2,1)} %all-to-all-done.refs_0_, bf16[96,128,128]{2,1,0:T(8,128)(2,1)} %refs_4_.7), custom_call_target="tpu_custom_call" | custom-call | tf_op jit(solution)/shard_map/tiles/pallas_call | solution.py:113
  78.8 3.3 collective-permute-start
  85.5 4.3 collective-permute-done
  89.8 5.2 %collective-permute-done.1 = bf16[4,128,256]{2,1,0:T(8,128)(2,1)S(1)} collective-permute-done((bf16[4,128,256]{2,1,0:T(8,128)(2,1)}, bf16[4,128,256]{2,1,0:T(8,128)(2,1)S(1)}, u32[]{:S(2)}, u32[]{:S(2)}) %collective-permute-start.1) | collective-permute-done | bytes 262176 | tf_op jit(solution)/shard_map/ppermute | solution.py:197
  102.5 5.7 %all-to-all-start.3 = ((bf16[32,128,256]{2,1,0:T(8,128)(2,1)}), bf16[32,128,256]{2,1,0:T(8,128)(2,1)}, u32[]{:S(2)}, u32[]{:S(2)}) async-start(bf16[32,128,256]{2,1,0:T(8,128)(2,1)} %pick.7), calls=%async_computation.3 | async-start | bytes 4194304 | tf_op jit(solution)/shard_map/all_to_all | solution.py:22
  110.9 23.7 %all-to-all-done.3.refs_0_ = bf16[32,128,256]{2,1,0:T(8,128)(2,1)} async-done(((bf16[32,128,256]{2,1,0:T(8,128)(2,1)}), bf16[32,128,256]{2,1,0:T(8,128)(2,1)}, u32[]{:S(2)}, u32[]{:S(2)}) %all-to-all-start.3) | async-done | bytes 2097184 | tf_op jit(solution)/shard_map/all_to_all | solution.py:22
  134.6 8.4 %all-to-all-start.2 = ((bf16[32,128,256]{2,1,0:T(8,128)(2,1)}), bf16[32,128,256]{2,1,0:T(8,128)(2,1)}, u32[]{:S(2)}, u32[]{:S(2)}) async-start(bf16[32,128,256]{2,1,0:T(8,128)(2,1)} %pick.6), calls=%async_computation.2 | async-start | bytes 4194304 | tf_op jit(solution)/shard_map/all_to_all | solution.py:22
  143.2 6.2 %tiles.7 = (bf16[4,128,256]{2,1,0:T(8,128)(2,1)}, bf16[4,128,256]{2,1,0:T(8,128)(2,1)}, bf16[4,128,256]{2,1,0:T(8,128)(2,1)}, bf16[4,128,256]{2,1,0:T(8,128)(2,1)}) custom-call(s32[337]{0:T(512)} %concatenate.25.table, bf16[32,128,256]{2,1,0:T(8,128)(2,1)} %all-to-all-done.3.refs_0_, bf16[96,128,128]{2,1,0:T(8,128)(2,1)} %refs_4_.7), custom_call_target="tpu_custom_call" | custom-call | tf_op jit(solution)/shard_map/tiles/pallas_call | solution.py:113
  156.8 12.9 %all-to-all-done.2.refs_0_ = bf16[32,128,256]{2,1,0:T(8,128)(2,1)} async-done(((bf16[32,128,256]{2,1,0:T(8,128)(2,1)}), bf16[32,128,256]{2,1,0:T(8,128)(2,1)}, u32[]{:S(2)}, u32[]{:S(2)}) %all-to-all-start.2) | async-done | bytes 2097184 | tf_op jit(solution)/shard_map/all_to_all | solution.py:22
  169.7 6.1 %tiles.6 = (bf16[4,128,256]{2,1,0:T(8,128)(2,1)}, bf16[4,128,256]{2,1,0:T(8,128)(2,1)}, bf16[4,128,256]{2,1,0:T(8,128)(2,1)}, bf16[4,128,256]{2,1,0:T(8,128)(2,1)}) custom-call(s32[337]{0:T(512)} %concatenate.25.table, bf16[32,128,256]{2,1,0:T(8,128)(2,1)} %all-to-all-done.2.refs_0_, bf16[96,128,128]{2,1,0:T(8,128)(2,1)} %refs_4_.7), custom_call_target="tpu_custom_call" | custom-call | tf_op jit(solution)/shard_map/tiles/pallas_call | solution.py:113
  181.4 5.5 %collective-permute-done.6 = bf16[4,128,256]{2,1,0:T(8,128)(2,1)S(1)} collective-permute-done((bf16[4,128,256]{2,1,0:T(8,128)(2,1)}, bf16[4,128,256]{2,1,0:T(8,128)(2,1)S(1)}, u32[]{:S(2)}, u32[]{:S(2)}) %collective-permute-start.6) | collective-permute-done | bytes 262176 | tf_op jit(solution)/shard_map/ppermute | solution.py:197
  186.9 5.0 %collective-permute-done.7 = bf16[4,128,256]{2,1,0:T(8,128)(2,1)S(1)} collective-permute-done((bf16[4,128,256]{2,1,0:T(8,128)(2,1)}, bf16[4,128,256]{2,1,0:T(8,128)(2,1)S(1)}, u32[]{:S(2)}, u32[]{:S(2)}) %collective-permute-start.7) | collective-permute-done | bytes 262176 | tf_op jit(solution)/shard_map/ppermute | solution.py:197
  201.6 3.0 collective-permute-start.16
  213.8 4.8 %all-to-all-start.10 = ((bf16[2,64,64,128]{3,2,1,0:T(8,128)(2,1)}), bf16[2,64,64,128]{3,2,1,0:T(8,128)(2,1)}, u32[]{:S(2)}, u32[]{:S(2)}) async-start(bf16[2,64,64,128]{3,2,1,0:T(8,128)(2,1)} %copy_bitcast_fusion), calls=%async_computation.10 | async-start | bytes 4194304 | tf_op jit(solution)/shard_map/all_to_all | solution.py:22
  219.3 6.9 %tiles_t.5 = bf16[32,128,256]{2,1,0:T(8,128)(2,1)} custom-call(s32[385]{0:T(512)} %concatenate.24.table, bf16[4,128,256]{2,1,0:T(8,128)(2,1)} %copy-done.12, bf16[4,128,256]{2,1,0:T(8,128)(2,1)} %collective-permute-done.15.refs_1_, bf16[4,128,256]{2,1,0:T(8,128)(2,1)} %collective-permute-done.16.refs_2_, bf16[4,128,256]{2,1,0:T(8,128)(2,1)} %copy-done.16, ...), custom_call_target="tpu_custom_call" | custom-call | tf_op jit(solution)/shard_map/tiles_t/pallas_call | solution.py:113
  226.3 6.0 %all-to-all-start.5 = ((bf16[32,128,256]{2,1,0:T(8,128)(2,1)}), bf16[32,128,256]{2,1,0:T(8,128)(2,1)}, u32[]{:S(2)}, u32[]{:S(2)}) async-start(bf16[32,128,256]{2,1,0:T(8,128)(2,1)} %tiles_t.5), calls=%async_computation.5 | async-start | bytes 4194304 | tf_op jit(solution)/shard_map/all_to_all | solution.py:22
  237.5 4.9 %collective-permute-done.14.refs_3_ = bf16[4,128,256]{2,1,0:T(8,128)(2,1)S(1)} collective-permute-done((bf16[4,128,256]{2,1,0:T(8,128)(2,1)S(1)}, bf16[4,128,256]{2,1,0:T(8,128)(2,1)S(1)}, u32[]{:S(2)}, u32[]{:S(2)}) %collective-permute-start.14) | collective-permute-done | bytes 262176 | tf_op jit(solution)/shard_map/ppermute | solution.py:197
  242.4 5.6 %collective-permute-done.13.refs_2_ = bf16[4,128,256]{2,1,0:T(8,128)(2,1)S(1)} collective-permute-done((bf16[4,128,256]{2,1,0:T(8,128)(2,1)S(1)}, bf16[4,128,256]{2,1,0:T(8,128)(2,1)S(1)}, u32[]{:S(2)}, u32[]{:S(2)}) %collective-permute-start.13) | collective-permute-done | bytes 262176 | tf_op jit(solution)/shard_map/ppermute | solution.py:197
  249.3 7.0 %tiles_t.4 = bf16[32,128,256]{2,1,0:T(8,128)(2,1)} custom-call(s32[385]{0:T(512)} %concatenate.24.table, bf16[4,128,256]{2,1,0:T(8,128)(2,1)} %copy-done.10, bf16[4,128,256]{2,1,0:T(8,128)(2,1)} %copy-done.23, bf16[4,128,256]{2,1,0:T(8,128)(2,1)} %copy-done.21, bf16[4,128,256]{2,1,0:T(8,128)(2,1)} %copy-done.18, bf16[96,128,128]{2,1,0:T(8,128)(2,1)} %refs_4_.7), custom_call_target="tpu_custom_call" | custom-call | tf_op jit(solution)/shard_map/tiles_t/pallas_call | solution.py:113
  256.3 3.0 all-to-all-done.5.returned
  259.3 7.8 %all-to-all-start.4 = ((bf16[32,128,256]{2,1,0:T(8,128)(2,1)}), bf16[32,128,256]{2,1,0:T(8,128)(2,1)}, u32[]{:S(2)}, u32[]{:S(2)}) async-start(bf16[32,128,256]{2,1,0:T(8,128)(2,1)} %tiles_t.4), calls=%async_computation.4 | async-start | bytes 4194304 | tf_op jit(solution)/shard_map/all_to_all | solution.py:22
  267.2 3.4 reduce_sum.204
  270.5 2.9 place.5
  273.5 20.4 %all-to-all-done.4.returned = bf16[32,128,256]{2,1,0:T(8,128)(2,1)} async-done(((bf16[32,128,256]{2,1,0:T(8,128)(2,1)}), bf16[32,128,256]{2,1,0:T(8,128)(2,1)}, u32[]{:S(2)}, u32[]{:S(2)}) %all-to-all-start.4) | async-done | bytes 2097184 | tf_op jit(solution)/shard_map/all_to_all | solution.py:22
  297.8 4.2 multiply_convert_fusion.1
  305.5 3.0 convolution_convert_fusion.3
  312.3 6.5 %all_to_all.60 = bf16[2,64,64,128]{3,2,1,0:T(8,128)(2,1)} all-to-all(bf16[2,64,64,128]{3,2,1,0:T(8,128)(2,1)S(1)} %copy_bitcast_fusion.1), channel_id=1, replica_groups=mesh['grp'=4,'row_0'=4,'row_1'=4,'row_2'=2] {'row_2'}, dimensions={0} | all-to-all | bytes 4194304 | tf_op jit(solution)/shard_map/all_to_all | solution.py:22
  318.8 8.4 %all-to-all-start.11 = ((bf16[64,64,128]{2,1,0:T(8,128)(2,1)}), bf16[64,64,128]{2,1,0:T(8,128)(2,1)S(1)}, u32[]{:S(2)}, u32[]{:S(2)}) async-start(bf16[64,64,128]{2,1,0:T(8,128)(2,1)} %reduce_sum.204), calls=%async_computation.11 | async-start | bytes 2097152 | tf_op jit(solution)/shard_map/all_to_all | solution.py:22
  327.2 3.4 reduce_sum.202
  330.6 3.3 multiply_reduce_fusion
  333.8 11.7 %all-to-all-done.11 = bf16[64,64,128]{2,1,0:T(8,128)(2,1)S(1)} async-done(((bf16[64,64,128]{2,1,0:T(8,128)(2,1)}), bf16[64,64,128]{2,1,0:T(8,128)(2,1)S(1)}, u32[]{:S(2)}, u32[]{:S(2)}) %all-to-all-start.11) | async-done | bytes 1048608 | tf_op jit(solution)/shard_map/all_to_all | solution.py:22
  345.5 6.2 %all-to-all-start.9 = ((bf16[64,64,128]{2,1,0:T(8,128)(2,1)}), bf16[64,64,128]{2,1,0:T(8,128)(2,1)}, u32[]{:S(2)}, u32[]{:S(2)}) async-start(bf16[64,64,128]{2,1,0:T(8,128)(2,1)} %reduce_sum.202), calls=%async_computation.9 | async-start | bytes 2097152 | tf_op jit(solution)/shard_map/all_to_all | solution.py:22
  360.2 12.2 %collective-permute-done.23.refs_3_ = bf16[4,128,256]{2,1,0:T(8,128)(2,1)S(1)} collective-permute-done((bf16[4,128,256]{2,1,0:T(8,128)(2,1)S(1)}, bf16[4,128,256]{2,1,0:T(8,128)(2,1)S(1)}, u32[]{:S(2)}, u32[]{:S(2)}) %collective-permute-start.23) | collective-permute-done | bytes 262176 | tf_op jit(solution)/shard_map/ppermute | solution.py:197
  372.4 4.7 %collective-permute-done.22.refs_2_ = bf16[4,128,256]{2,1,0:T(8,128)(2,1)S(1)} collective-permute-done((bf16[4,128,256]{2,1,0:T(8,128)(2,1)S(1)}, bf16[4,128,256]{2,1,0:T(8,128)(2,1)S(1)}, u32[]{:S(2)}, u32[]{:S(2)}) %collective-permute-start.22) | collective-permute-done | bytes 262176 | tf_op jit(solution)/shard_map/ppermute | solution.py:197
  378.5 6.9 %tiles_t.7 = bf16[32,128,256]{2,1,0:T(8,128)(2,1)} custom-call(s32[385]{0:T(512)} %concatenate.24.table, bf16[4,128,256]{2,1,0:T(8,128)(2,1)} %copy-done.13, bf16[4,128,256]{2,1,0:T(8,128)(2,1)} %copy-done.24, bf16[4,128,256]{2,1,0:T(8,128)(2,1)} %copy-done.22, bf16[4,128,256]{2,1,0:T(8,128)(2,1)} %copy-done.19, bf16[96,128,128]{2,1,0:T(8,128)(2,1)} %refs_4_.7), custom_call_target="tpu_custom_call" | custom-call | tf_op jit(solution)/shard_map/tiles_t/pallas_call | solution.py:113
  385.4 6.7 %all-to-all-start.7 = ((bf16[32,128,256]{2,1,0:T(8,128)(2,1)}), bf16[32,128,256]{2,1,0:T(8,128)(2,1)S(1)}, u32[]{:S(2)}, u32[]{:S(2)}) async-start(bf16[32,128,256]{2,1,0:T(8,128)(2,1)} %tiles_t.7), calls=%async_computation.7 | async-start | bytes 4194304 | tf_op jit(solution)/shard_map/all_to_all | solution.py:22
  395.5 11.9 %collective-permute-done.20.refs_3_ = bf16[4,128,256]{2,1,0:T(8,128)(2,1)S(1)} collective-permute-done((bf16[4,128,256]{2,1,0:T(8,128)(2,1)S(1)}, bf16[4,128,256]{2,1,0:T(8,128)(2,1)S(1)}, u32[]{:S(2)}, u32[]{:S(2)}) %collective-permute-start.20) | collective-permute-done | bytes 262176 | tf_op jit(solution)/shard_map/ppermute | solution.py:197
  408.8 6.9 %tiles_t.6 = bf16[32,128,256]{2,1,0:T(8,128)(2,1)} custom-call(s32[385]{0:T(512)} %concatenate.24.table, bf16[4,128,256]{2,1,0:T(8,128)(2,1)} %copy-done.11, bf16[4,128,256]{2,1,0:T(8,128)(2,1)} %collective-permute-done.18.refs_1_, bf16[4,128,256]{2,1,0:T(8,128)(2,1)} %copy-done.20, bf16[4,128,256]{2,1,0:T(8,128)(2,1)} %copy-done.17, ...), custom_call_target="tpu_custom_call" | custom-call | tf_op jit(solution)/shard_map/tiles_t/pallas_call | solution.py:113
  415.7 3.1 all-to-all-done.7.returned
  420.1 8.1 %all-to-all-start.6 = ((bf16[32,128,256]{2,1,0:T(8,128)(2,1)}), bf16[32,128,256]{2,1,0:T(8,128)(2,1)}, u32[]{:S(2)}, u32[]{:S(2)}) async-start(bf16[32,128,256]{2,1,0:T(8,128)(2,1)} %tiles_t.6), calls=%async_computation.6 | async-start | bytes 4194304 | tf_op jit(solution)/shard_map/all_to_all | solution.py:22
  431.1 2.9 place.7
  434.0 20.9 %all-to-all-done.6.returned = bf16[32,128,256]{2,1,0:T(8,128)(2,1)} async-done(((bf16[32,128,256]{2,1,0:T(8,128)(2,1)}), bf16[32,128,256]{2,1,0:T(8,128)(2,1)}, u32[]{:S(2)}, u32[]{:S(2)}) %all-to-all-start.6) | async-done | bytes 2097184 | tf_op jit(solution)/shard_map/all_to_all | solution.py:22
  (168 shorter events, 99.4 us)
Async XLA Ops:
  3.2 34.7 %all-to-all-start.1 = ((bf16[32,128,256]{2,1,0:T(8,128)(2,1)}), bf16[32,128,256]{2,1,0:T(8,128)(2,1)S(1)}, u32[]{:S(2)}, u32[]{:S(2)}) async-start(bf16[32,128,256]{2,1,0:T(8,128)(2,1)} %pick.5), calls=%async_computation.1 | async-start | bytes 4194304 | tf_op jit(solution)/shard_map/all_to_all | solution.py:22
  15.7 30.3 %copy-start.28 = (s32[96]{0:T(128)S(1)}, s32[96]{0:T(128)}, u32[]{:S(2)}) copy-start(s32[96]{0:T(128)} %param.11) | copy-start | bytes 1156
  37.9 34.8 %all-to-all-start = ((bf16[32,128,256]{2,1,0:T(8,128)(2,1)}), bf16[32,128,256]{2,1,0:T(8,128)(2,1)}, u32[]{:S(2)}, u32[]{:S(2)}) async-start(bf16[32,128,256]{2,1,0:T(8,128)(2,1)} %pick.4), calls=%async_computation | async-start | bytes 4194304 | tf_op jit(solution)/shard_map/all_to_all | solution.py:22
  56.2 26.6 %collective-permute-start.3 = (bf16[4,128,256]{2,1,0:T(8,128)(2,1)}, bf16[4,128,256]{2,1,0:T(8,128)(2,1)S(1)}, u32[]{:S(2)}, u32[]{:S(2)}) collective-permute-start(bf16[4,128,256]{2,1,0:T(8,128)(2,1)} %get-tuple-element.24), channel_id=1, source_target_pairs={{0,64},{32,96},{64,0},{96,32},{1,65},{33,97},{65,1},{97,33},{2,66}... | collective-permute-start | bytes 786440 | tf_op jit(solution)/shard_map/ppermute | solution.py:197
  59.5 25.9 %collective-permute-start.4 = (bf16[4,128,256]{2,1,0:T(8,128)(2,1)}, bf16[4,128,256]{2,1,0:T(8,128)(2,1)S(1)}, u32[]{:S(2)}, u32[]{:S(2)}) collective-permute-start(bf16[4,128,256]{2,1,0:T(8,128)(2,1)} %get-tuple-element.25), channel_id=1, source_target_pairs={{0,32},{32,64},{64,96},{96,0},{1,33},{33,65},{65,97},{97,1},{2,34}... | collective-permute-start | bytes 786440 | tf_op jit(solution)/shard_map/ppermute | solution.py:197
  60.1 25.2 %copy-start.26 = (bf16[4,128,256]{2,1,0:T(8,128)(2,1)S(1)}, bf16[4,128,256]{2,1,0:T(8,128)(2,1)}, u32[]{:S(2)}) copy-start(bf16[4,128,256]{2,1,0:T(8,128)(2,1)} %get-tuple-element.23) | copy-start | bytes 786436
  60.2 25.2 %collective-permute-start.5 = (bf16[4,128,256]{2,1,0:T(8,128)(2,1)}, bf16[4,128,256]{2,1,0:T(8,128)(2,1)S(1)}, u32[]{:S(2)}, u32[]{:S(2)}) collective-permute-start(bf16[4,128,256]{2,1,0:T(8,128)(2,1)} %get-tuple-element.26), channel_id=1, source_target_pairs={{0,96},{32,0},{64,32},{96,64},{1,97},{33,1},{65,33},{97,65},{2,98}... | collective-permute-start | bytes 786440 | tf_op jit(solution)/shard_map/ppermute | solution.py:197
  78.8 17.8 %copy-start = (bf16[512,512]{1,0:T(8,128)(2,1)S(1)}, bf16[512,512]{1,0:T(8,128)(2,1)}, u32[]{:S(2)}) copy-start(bf16[512,512]{1,0:T(8,128)(2,1)} %param.9) | copy-start | bytes 1572868
  78.8 11.0 %collective-permute-start = (bf16[4,128,256]{2,1,0:T(8,128)(2,1)}, bf16[4,128,256]{2,1,0:T(8,128)(2,1)S(1)}, u32[]{:S(2)}, u32[]{:S(2)}) collective-permute-start(bf16[4,128,256]{2,1,0:T(8,128)(2,1)} %get-tuple-element.20), channel_id=1, source_target_pairs={{0,64},{32,96},{64,0},{96,32},{1,65},{33,97},{65,1},{97,33},{2,66}... | collective-permute-start | bytes 786440 | tf_op jit(solution)/shard_map/ppermute | solution.py:197
  82.1 13.0 %collective-permute-start.1 = (bf16[4,128,256]{2,1,0:T(8,128)(2,1)}, bf16[4,128,256]{2,1,0:T(8,128)(2,1)S(1)}, u32[]{:S(2)}, u32[]{:S(2)}) collective-permute-start(bf16[4,128,256]{2,1,0:T(8,128)(2,1)} %get-tuple-element.21), channel_id=1, source_target_pairs={{0,32},{32,64},{64,96},{96,0},{1,33},{33,65},{65,97},{97,1},{2,34}... | collective-permute-start | bytes 786440 | tf_op jit(solution)/shard_map/ppermute | solution.py:197
  82.8 12.7 %collective-permute-start.2 = (bf16[4,128,256]{2,1,0:T(8,128)(2,1)}, bf16[4,128,256]{2,1,0:T(8,128)(2,1)S(1)}, u32[]{:S(2)}, u32[]{:S(2)}) collective-permute-start(bf16[4,128,256]{2,1,0:T(8,128)(2,1)} %get-tuple-element.22), channel_id=1, source_target_pairs={{0,96},{32,0},{64,32},{96,64},{1,97},{33,1},{65,33},{97,65},{2,98}... | collective-permute-start | bytes 786440 | tf_op jit(solution)/shard_map/ppermute | solution.py:197
  85.3 11.5 %copy-start.8 = (bf16[2,512,1024]{2,1,0:T(8,128)(2,1)S(1)}, bf16[2,512,1024]{2,1,0:T(8,128)(2,1)}, u32[]{:S(2)}) copy-start(bf16[2,512,1024]{2,1,0:T(8,128)(2,1)} %param.15) | copy-start | bytes 6291460
  102.5 32.1 %all-to-all-start.3 = ((bf16[32,128,256]{2,1,0:T(8,128)(2,1)}), bf16[32,128,256]{2,1,0:T(8,128)(2,1)}, u32[]{:S(2)}, u32[]{:S(2)}) async-start(bf16[32,128,256]{2,1,0:T(8,128)(2,1)} %pick.7), calls=%async_computation.3 | async-start | bytes 4194304 | tf_op jit(solution)/shard_map/all_to_all | solution.py:22
  134.6 35.1 %all-to-all-start.2 = ((bf16[32,128,256]{2,1,0:T(8,128)(2,1)}), bf16[32,128,256]{2,1,0:T(8,128)(2,1)}, u32[]{:S(2)}, u32[]{:S(2)}) async-start(bf16[32,128,256]{2,1,0:T(8,128)(2,1)} %pick.6), calls=%async_computation.2 | async-start | bytes 4194304 | tf_op jit(solution)/shard_map/all_to_all | solution.py:22
  149.4 30.2 %collective-permute-start.9 = (bf16[4,128,256]{2,1,0:T(8,128)(2,1)}, bf16[4,128,256]{2,1,0:T(8,128)(2,1)S(1)}, u32[]{:S(2)}, u32[]{:S(2)}) collective-permute-start(bf16[4,128,256]{2,1,0:T(8,128)(2,1)} %get-tuple-element.32), channel_id=1, source_target_pairs={{0,64},{32,96},{64,0},{96,32},{1,65},{33,97},{65,1},{97,33},{2,66}... | collective-permute-start | bytes 786440 | tf_op jit(solution)/shard_map/ppermute | solution.py:197
  151.5 29.7 %collective-permute-start.10 = (bf16[4,128,256]{2,1,0:T(8,128)(2,1)}, bf16[4,128,256]{2,1,0:T(8,128)(2,1)S(1)}, u32[]{:S(2)}, u32[]{:S(2)}) collective-permute-start(bf16[4,128,256]{2,1,0:T(8,128)(2,1)} %get-tuple-element.33), channel_id=1, source_target_pairs={{0,32},{32,64},{64,96},{96,0},{1,33},{33,65},{65,97},{97,1},{2,34}... | collective-permute-start | bytes 786440 | tf_op jit(solution)/shard_map/ppermute | solution.py:197
  153.1 28.1 %collective-permute-start.11 = (bf16[4,128,256]{2,1,0:T(8,128)(2,1)}, bf16[4,128,256]{2,1,0:T(8,128)(2,1)S(1)}, u32[]{:S(2)}, u32[]{:S(2)}) collective-permute-start(bf16[4,128,256]{2,1,0:T(8,128)(2,1)} %get-tuple-element.34), channel_id=1, source_target_pairs={{0,96},{32,0},{64,32},{96,64},{1,97},{33,1},{65,33},{97,65},{2,98}... | collective-permute-start | bytes 786440 | tf_op jit(solution)/shard_map/ppermute | solution.py:197
  156.8 24.4 %copy-start.25 = (bf16[4,128,256]{2,1,0:T(8,128)(2,1)S(1)}, bf16[4,128,256]{2,1,0:T(8,128)(2,1)}, u32[]{:S(2)}) copy-start(bf16[4,128,256]{2,1,0:T(8,128)(2,1)} %get-tuple-element.31) | copy-start | bytes 786436
  175.8 17.6 %copy-start.1 = (bf16[512,512]{1,0:T(8,128)(2,1)S(1)}, bf16[512,512]{1,0:T(8,128)(2,1)}, u32[]{:S(2)}) copy-start(bf16[512,512]{1,0:T(8,128)(2,1)} %fusion) | copy-start | bytes 1572868
  175.9 11.0 %collective-permute-start.6 = (bf16[4,128,256]{2,1,0:T(8,128)(2,1)}, bf16[4,128,256]{2,1,0:T(8,128)(2,1)S(1)}, u32[]{:S(2)}, u32[]{:S(2)}) collective-permute-start(bf16[4,128,256]{2,1,0:T(8,128)(2,1)} %get-tuple-element.28), channel_id=1, source_target_pairs={{0,64},{32,96},{64,0},{96,32},{1,65},{33,97},{65,1},{97,33},{2,66}... | collective-permute-start | bytes 786440 | tf_op jit(solution)/shard_map/ppermute | solution.py:197
  178.0 13.9 %collective-permute-start.7 = (bf16[4,128,256]{2,1,0:T(8,128)(2,1)}, bf16[4,128,256]{2,1,0:T(8,128)(2,1)S(1)}, u32[]{:S(2)}, u32[]{:S(2)}) collective-permute-start(bf16[4,128,256]{2,1,0:T(8,128)(2,1)} %get-tuple-element.29), channel_id=1, source_target_pairs={{0,32},{32,64},{64,96},{96,0},{1,33},{33,65},{65,97},{97,1},{2,34}... | collective-permute-start | bytes 786440 | tf_op jit(solution)/shard_map/ppermute | solution.py:197
  179.6 12.7 %collective-permute-start.8 = (bf16[4,128,256]{2,1,0:T(8,128)(2,1)}, bf16[4,128,256]{2,1,0:T(8,128)(2,1)S(1)}, u32[]{:S(2)}, u32[]{:S(2)}) collective-permute-start(bf16[4,128,256]{2,1,0:T(8,128)(2,1)} %get-tuple-element.30), channel_id=1, source_target_pairs={{0,96},{32,0},{64,32},{96,64},{1,97},{33,1},{65,33},{97,65},{2,98}... | collective-permute-start | bytes 786440 | tf_op jit(solution)/shard_map/ppermute | solution.py:197
  181.2 12.4 %copy-start.9 = (bf16[2,512,1024]{2,1,0:T(8,128)(2,1)S(1)}, bf16[2,512,1024]{2,1,0:T(8,128)(2,1)}, u32[]{:S(2)}) copy-start(bf16[2,512,1024]{2,1,0:T(8,128)(2,1)} %param.15) | copy-start | bytes 6291460
  200.4 8.2 %copy-start.12 = (bf16[4,128,256]{2,1,0:T(8,128)(2,1)}, bf16[4,128,256]{2,1,0:T(8,128)(2,1)S(1)}, u32[]{:S(2)}) copy-start(bf16[4,128,256]{2,1,0:T(8,128)(2,1)S(1)} %get-tuple-element.54.refs_0_) | copy-start | bytes 786436
  200.4 35.6 %copy-start.10 = (bf16[4,128,256]{2,1,0:T(8,128)(2,1)}, bf16[4,128,256]{2,1,0:T(8,128)(2,1)S(1)}, u32[]{:S(2)}) copy-start(bf16[4,128,256]{2,1,0:T(8,128)(2,1)S(1)} %get-tuple-element.53.refs_0_) | copy-start | bytes 786436
  200.4 18.2 %collective-permute-start.17 = (bf16[4,128,256]{2,1,0:T(8,128)(2,1)S(1)}, bf16[4,128,256]{2,1,0:T(8,128)(2,1)S(1)}, u32[]{:S(2)}, u32[]{:S(2)}) collective-permute-start(bf16[4,128,256]{2,1,0:T(8,128)(2,1)S(1)} %get-tuple-element.54.refs_0_), channel_id=1, source_target_pairs={{0,32},{32,64},{64,96},{96,0},{1,33},{33,65},{65,97},{97,1},{2,34}... | collective-permute-start | bytes 786440 | tf_op jit(solution)/shard_map/ppermute | solution.py:197
  201.6 17.0 %collective-permute-start.16 = (bf16[4,128,256]{2,1,0:T(8,128)(2,1)S(1)}, bf16[4,128,256]{2,1,0:T(8,128)(2,1)}, u32[]{:S(2)}, u32[]{:S(2)}) collective-permute-start(bf16[4,128,256]{2,1,0:T(8,128)(2,1)S(1)} %get-tuple-element.54.refs_0_), channel_id=1, source_target_pairs={{0,64},{32,96},{64,0},{96,32},{1,65},{33,97},{65,1},{97,33},{2,66}... | collective-permute-start | bytes 786440 | tf_op jit(solution)/shard_map/ppermute | solution.py:197
  204.6 14.1 %collective-permute-start.15 = (bf16[4,128,256]{2,1,0:T(8,128)(2,1)S(1)}, bf16[4,128,256]{2,1,0:T(8,128)(2,1)}, u32[]{:S(2)}, u32[]{:S(2)}) collective-permute-start(bf16[4,128,256]{2,1,0:T(8,128)(2,1)S(1)} %get-tuple-element.54.refs_0_), channel_id=1, source_target_pairs={{0,96},{32,0},{64,32},{96,64},{1,97},{33,1},{65,33},{97,65},{2,98}... | collective-permute-start | bytes 786440 | tf_op jit(solution)/shard_map/ppermute | solution.py:197
  213.8 12.5 %all-to-all-start.10 = ((bf16[2,64,64,128]{3,2,1,0:T(8,128)(2,1)}), bf16[2,64,64,128]{3,2,1,0:T(8,128)(2,1)}, u32[]{:S(2)}, u32[]{:S(2)}) async-start(bf16[2,64,64,128]{3,2,1,0:T(8,128)(2,1)} %copy_bitcast_fusion), calls=%async_computation.10 | async-start | bytes 4194304 | tf_op jit(solution)/shard_map/all_to_all | solution.py:22
  226.3 33.0 %all-to-all-start.5 = ((bf16[32,128,256]{2,1,0:T(8,128)(2,1)}), bf16[32,128,256]{2,1,0:T(8,128)(2,1)}, u32[]{:S(2)}, u32[]{:S(2)}) async-start(bf16[32,128,256]{2,1,0:T(8,128)(2,1)} %tiles_t.5), calls=%async_computation.5 | async-start | bytes 4194304 | tf_op jit(solution)/shard_map/all_to_all | solution.py:22
  232.3 10.1 %collective-permute-start.14 = (bf16[4,128,256]{2,1,0:T(8,128)(2,1)S(1)}, bf16[4,128,256]{2,1,0:T(8,128)(2,1)S(1)}, u32[]{:S(2)}, u32[]{:S(2)}) collective-permute-start(bf16[4,128,256]{2,1,0:T(8,128)(2,1)S(1)} %get-tuple-element.53.refs_0_), channel_id=1, source_target_pairs={{0,32},{32,64},{64,96},{96,0},{1,33},{33,65},{65,97},{97,1},{2,34}... | collective-permute-start | bytes 786440 | tf_op jit(solution)/shard_map/ppermute | solution.py:197
  234.4 13.6 %collective-permute-start.13 = (bf16[4,128,256]{2,1,0:T(8,128)(2,1)S(1)}, bf16[4,128,256]{2,1,0:T(8,128)(2,1)S(1)}, u32[]{:S(2)}, u32[]{:S(2)}) collective-permute-start(bf16[4,128,256]{2,1,0:T(8,128)(2,1)S(1)} %get-tuple-element.53.refs_0_), channel_id=1, source_target_pairs={{0,64},{32,96},{64,0},{96,32},{1,65},{33,97},{65,1},{97,33},{2,66}... | collective-permute-start | bytes 786440 | tf_op jit(solution)/shard_map/ppermute | solution.py:197
  236.0 12.1 %collective-permute-start.12 = (bf16[4,128,256]{2,1,0:T(8,128)(2,1)S(1)}, bf16[4,128,256]{2,1,0:T(8,128)(2,1)S(1)}, u32[]{:S(2)}, u32[]{:S(2)}) collective-permute-start(bf16[4,128,256]{2,1,0:T(8,128)(2,1)S(1)} %get-tuple-element.53.refs_0_), channel_id=1, source_target_pairs={{0,96},{32,0},{64,32},{96,64},{1,97},{33,1},{65,33},{97,65},{2,98}... | collective-permute-start | bytes 786440 | tf_op jit(solution)/shard_map/ppermute | solution.py:197
  259.3 34.5 %all-to-all-start.4 = ((bf16[32,128,256]{2,1,0:T(8,128)(2,1)}), bf16[32,128,256]{2,1,0:T(8,128)(2,1)}, u32[]{:S(2)}, u32[]{:S(2)}) async-start(bf16[32,128,256]{2,1,0:T(8,128)(2,1)} %tiles_t.4), calls=%async_computation.4 | async-start | bytes 4194304 | tf_op jit(solution)/shard_map/all_to_all | solution.py:22
  273.5 23.3 %copy-start.15 = (bf16[4,128,256]{2,1,0:T(8,128)(2,1)S(1)}, bf16[4,128,256]{2,1,0:T(8,128)(2,1)}, u32[]{:S(2)}) copy-start(bf16[4,128,256]{2,1,0:T(8,128)(2,1)} %place.5) | copy-start | bytes 786436
  318.8 26.8 %all-to-all-start.11 = ((bf16[64,64,128]{2,1,0:T(8,128)(2,1)}), bf16[64,64,128]{2,1,0:T(8,128)(2,1)S(1)}, u32[]{:S(2)}, u32[]{:S(2)}) async-start(bf16[64,64,128]{2,1,0:T(8,128)(2,1)} %reduce_sum.204), calls=%async_computation.11 | async-start | bytes 2097152 | tf_op jit(solution)/shard_map/all_to_all | solution.py:22
  345.5 39.9 %all-to-all-start.9 = ((bf16[64,64,128]{2,1,0:T(8,128)(2,1)}), bf16[64,64,128]{2,1,0:T(8,128)(2,1)}, u32[]{:S(2)}, u32[]{:S(2)}) async-start(bf16[64,64,128]{2,1,0:T(8,128)(2,1)} %reduce_sum.202), calls=%async_computation.9 | async-start | bytes 2097152 | tf_op jit(solution)/shard_map/all_to_all | solution.py:22
  354.3 22.8 %copy-start.13 = (bf16[4,128,256]{2,1,0:T(8,128)(2,1)}, bf16[4,128,256]{2,1,0:T(8,128)(2,1)S(1)}, u32[]{:S(2)}) copy-start(bf16[4,128,256]{2,1,0:T(8,128)(2,1)S(1)} %get-tuple-element.52.refs_0_) | copy-start | bytes 786436
  354.3 39.1 %copy-start.11 = (bf16[4,128,256]{2,1,0:T(8,128)(2,1)}, bf16[4,128,256]{2,1,0:T(8,128)(2,1)S(1)}, u32[]{:S(2)}) copy-start(bf16[4,128,256]{2,1,0:T(8,128)(2,1)S(1)} %get-tuple-element.51.refs_0_) | copy-start | bytes 786436
  354.3 18.1 %collective-permute-start.23 = (bf16[4,128,256]{2,1,0:T(8,128)(2,1)S(1)}, bf16[4,128,256]{2,1,0:T(8,128)(2,1)S(1)}, u32[]{:S(2)}, u32[]{:S(2)}) collective-permute-start(bf16[4,128,256]{2,1,0:T(8,128)(2,1)S(1)} %get-tuple-element.52.refs_0_), channel_id=1, source_target_pairs={{0,32},{32,64},{64,96},{96,0},{1,33},{33,65},{65,97},{97,1},{2,34}... | collective-permute-start | bytes 786440 | tf_op jit(solution)/shard_map/ppermute | solution.py:197
  356.0 21.2 %collective-permute-start.22 = (bf16[4,128,256]{2,1,0:T(8,128)(2,1)S(1)}, bf16[4,128,256]{2,1,0:T(8,128)(2,1)S(1)}, u32[]{:S(2)}, u32[]{:S(2)}) collective-permute-start(bf16[4,128,256]{2,1,0:T(8,128)(2,1)S(1)} %get-tuple-element.52.refs_0_), channel_id=1, source_target_pairs={{0,64},{32,96},{64,0},{96,32},{1,65},{33,97},{65,1},{97,33},{2,66}... | collective-permute-start | bytes 786440 | tf_op jit(solution)/shard_map/ppermute | solution.py:197
  358.8 18.3 %collective-permute-start.21 = (bf16[4,128,256]{2,1,0:T(8,128)(2,1)S(1)}, bf16[4,128,256]{2,1,0:T(8,128)(2,1)S(1)}, u32[]{:S(2)}, u32[]{:S(2)}) collective-permute-start(bf16[4,128,256]{2,1,0:T(8,128)(2,1)S(1)} %get-tuple-element.52.refs_0_), channel_id=1, source_target_pairs={{0,96},{32,0},{64,32},{96,64},{1,97},{33,1},{65,33},{97,65},{2,98}... | collective-permute-start | bytes 786440 | tf_op jit(solution)/shard_map/ppermute | solution.py:197
  385.4 33.3 %all-to-all-start.7 = ((bf16[32,128,256]{2,1,0:T(8,128)(2,1)}), bf16[32,128,256]{2,1,0:T(8,128)(2,1)S(1)}, u32[]{:S(2)}, u32[]{:S(2)}) async-start(bf16[32,128,256]{2,1,0:T(8,128)(2,1)} %tiles_t.7), calls=%async_computation.7 | async-start | bytes 4194304 | tf_op jit(solution)/shard_map/all_to_all | solution.py:22
  392.1 15.2 %collective-permute-start.20 = (bf16[4,128,256]{2,1,0:T(8,128)(2,1)S(1)}, bf16[4,128,256]{2,1,0:T(8,128)(2,1)S(1)}, u32[]{:S(2)}, u32[]{:S(2)}) collective-permute-start(bf16[4,128,256]{2,1,0:T(8,128)(2,1)S(1)} %get-tuple-element.51.refs_0_), channel_id=1, source_target_pairs={{0,32},{32,64},{64,96},{96,0},{1,33},{33,65},{65,97},{97,1},{2,34}... | collective-permute-start | bytes 786440 | tf_op jit(solution)/shard_map/ppermute | solution.py:197
  392.2 15.1 %collective-permute-start.19 = (bf16[4,128,256]{2,1,0:T(8,128)(2,1)S(1)}, bf16[4,128,256]{2,1,0:T(8,128)(2,1)S(1)}, u32[]{:S(2)}, u32[]{:S(2)}) collective-permute-start(bf16[4,128,256]{2,1,0:T(8,128)(2,1)S(1)} %get-tuple-element.51.refs_0_), channel_id=1, source_target_pairs={{0,64},{32,96},{64,0},{96,32},{1,65},{33,97},{65,1},{97,33},{2,66}... | collective-permute-start | bytes 786440 | tf_op jit(solution)/shard_map/ppermute | solution.py:197
  393.4 15.4 %collective-permute-start.18 = (bf16[4,128,256]{2,1,0:T(8,128)(2,1)S(1)}, bf16[4,128,256]{2,1,0:T(8,128)(2,1)}, u32[]{:S(2)}, u32[]{:S(2)}) collective-permute-start(bf16[4,128,256]{2,1,0:T(8,128)(2,1)S(1)} %get-tuple-element.51.refs_0_), channel_id=1, source_target_pairs={{0,96},{32,0},{64,32},{96,64},{1,97},{33,1},{65,33},{97,65},{2,98}... | collective-permute-start | bytes 786440 | tf_op jit(solution)/shard_map/ppermute | solution.py:197
  420.1 34.8 %all-to-all-start.6 = ((bf16[32,128,256]{2,1,0:T(8,128)(2,1)}), bf16[32,128,256]{2,1,0:T(8,128)(2,1)}, u32[]{:S(2)}, u32[]{:S(2)}) async-start(bf16[32,128,256]{2,1,0:T(8,128)(2,1)} %tiles_t.6), calls=%async_computation.6 | async-start | bytes 4194304 | tf_op jit(solution)/shard_map/all_to_all | solution.py:22
  434.0 23.8 %copy-start.14 = (bf16[4,128,256]{2,1,0:T(8,128)(2,1)S(1)}, bf16[4,128,256]{2,1,0:T(8,128)(2,1)}, u32[]{:S(2)}) copy-start(bf16[4,128,256]{2,1,0:T(8,128)(2,1)} %place.7) | copy-start | bytes 786436
  (18 other events, 42.5 us)
